TPU v7x, 32 devices: a whole 2x2x4 slice. The times are simulated.
32 devices in a mesh: seq: 4 (over z), shard: 4 (over y, core), replica: 2 (over x).
Axes of the slice: x: 2, y: 2, z: 4, core: 2. Of those that a mesh axis runs over, the one named last changes fastest.
Arguments:
- tokens: bfloat16 [8, 2048, 768], P(('shard', 'replica'), 'seq'), may hold values from -6 to 6
- prefix_len: int32 [8], P(('shard', 'replica')), may hold values from 204 to 1024
- w_qkv: bfloat16 [768, 2304], P('shard'), may hold values from -0.3125 to 0.3125
- w_out: bfloat16 [768, 768], P('shard'), may hold values from -1.75 to 1.75
- w_up: bfloat16 [768, 3072], P('shard'), may hold values from -0.21875 to 0.21875
- w_down: bfloat16 [3072, 768], P('shard'), may hold values from -0.109375 to 0.109375
- conv_w: bfloat16 [3, 2304], P(None, 'shard'), may hold values from -3 to 3
- gain_attn: bfloat16 [768], P('shard'), may hold values from 0.25 to 1.75
- gain_ffn: bfloat16 [768], P('shard'), may hold values from 0.25 to 1.75
- cotangent: bfloat16 [8, 2048, 768], P(('shard', 'replica'), 'seq'), may hold values from -6 to 6
Outputs:
- output: bfloat16 [8, 2048, 768], P(('shard', 'replica'), 'seq')
- grad_input: bfloat16 [8, 2048, 768], P(('shard', 'replica'), 'seq')
- grad_qkv: float32 [768, 2304], P('shard')
- grad_out: float32 [768, 768], P('shard')
- grad_up: float32 [768, 3072], P('shard')
- grad_down: float32 [3072, 768], P('shard')
- grad_conv: float32 [3, 2304], P(None, 'shard')
- grad_gain_attn: float32 [768], P('shard')
- grad_gain_ffn: float32 [768], P('shard')
All inputs are finite; a program needn't handle non-finite values.
Results may differ from a plain program's by a relative error of at most 0.019.
Values may be sent and summed in bfloat16 or wider, within the bound.
A program may use at most 192 MiB of HBM per device.

v0:
```python
import jax
import jax.numpy as jnp
from jax import lax
from jax.sharding import PartitionSpec as P

HEADS = 12
HEAD_DIM = 64


def shifted(array, axis, by):
    peers = lax.axis_size(axis)
    pairs = [(i, i + by) for i in range(peers) if 0 <= i + by < peers]
    return lax.ppermute(array, axis, pairs)


def rms_scale(values):
    return lax.rsqrt(jnp.mean(values * values, axis=-1, keepdims=True) + 1e-06)


def split_heads(matrix):
    return matrix.reshape(matrix.shape[0], HEADS, HEAD_DIM).transpose(1, 0, 2)


def merge_heads(tensor):
    return tensor.transpose(1, 0, 2).reshape(tensor.shape[1], HEADS * HEAD_DIM)


def visible(query_pos, key_pos, prefix_end):
    causal = key_pos[None, :] <= query_pos[:, None]
    inside = (key_pos[None, :] < prefix_end) & (query_pos[:, None] < prefix_end)
    return causal | inside


def norm_back(values, scale_rows, gain, upstream):
    weighted = upstream * gain
    grad_gain = jnp.sum(upstream * values * scale_rows, axis=0)
    grad_values = scale_rows * weighted - values * scale_rows**3 * jnp.mean(
        weighted * values, axis=-1, keepdims=True
    )
    return (grad_values, grad_gain)


def per_device(
    tokens, prefix_len, w_qkv, w_out, w_up, w_down, conv_w, gain_attn, gain_ffn, cotangent
):
    scale = HEAD_DIM ** (-0.5)
    rows = tokens.shape[1]
    width = tokens.shape[2]
    local_pos = lax.axis_index("seq") * rows + jnp.arange(rows, dtype=jnp.int32)
    prefix_end = prefix_len[0]
    inputs = tokens[0].astype(jnp.float32)
    full_qkv, full_out, full_up, full_down, full_conv, full_gone, full_gtwo = (
        lax.all_gather(w_qkv, "shard", axis=0, tiled=True),
        lax.all_gather(w_out, "shard", axis=0, tiled=True),
        lax.all_gather(w_up, "shard", axis=0, tiled=True),
        lax.all_gather(w_down, "shard", axis=0, tiled=True),
        lax.all_gather(conv_w, "shard", axis=1, tiled=True),
        lax.all_gather(gain_attn, "shard", axis=0, tiled=True),
        lax.all_gather(gain_ffn, "shard", axis=0, tiled=True),
    )
    scale_one = rms_scale(inputs)
    normed_b = (inputs * scale_one * full_gone.astype(jnp.float32)).astype(jnp.bfloat16)
    projected = jnp.dot(normed_b, full_qkv, preferred_element_type=jnp.float32).astype(jnp.bfloat16)
    before = shifted(projected[rows - 2 :], "seq", 1)
    extended = jnp.concatenate([before, projected], 0).astype(jnp.float32)
    kernel = full_conv.astype(jnp.float32)
    mixed = (
        kernel[0] * extended[2:] + kernel[1] * extended[1 : rows + 1] + kernel[2] * extended[:rows]
    )
    mixed_b = mixed.astype(jnp.bfloat16)
    query_rows = mixed_b[:, :width]
    keys_loc = mixed_b[:, width : 2 * width]
    values_loc = mixed_b[:, 2 * width :]
    queries = split_heads(query_rows)
    keys_heads = split_heads(keys_loc)
    values_heads = split_heads(values_loc)
    start_state = (
        jnp.full((HEADS, rows), -1e30, jnp.float32),
        jnp.zeros((HEADS, rows), jnp.float32),
        jnp.zeros((HEADS, rows, HEAD_DIM), jnp.float32),
    )
    key_piece = lax.all_gather(keys_loc, "seq", axis=0, tiled=True)
    value_piece = lax.all_gather(values_loc, "seq", axis=0, tiled=True)
    count = key_piece.shape[0]
    allowed = visible(local_pos, jnp.arange(count, dtype=jnp.int32), prefix_end)

    def per_head(items):
        query_h, key_h, value_h, running, total, accum = items
        scores = jnp.dot(query_h, key_h.T, preferred_element_type=jnp.float32) * scale
        scores = jnp.where(allowed, scores, -1e30)
        newmax = jnp.maximum(running, jnp.max(scores, axis=-1))
        factor = jnp.exp(running - newmax)
        weights = jnp.where(allowed, jnp.exp(scores - newmax[:, None]), 0.0)
        total = factor * total + jnp.sum(weights, axis=-1)
        accum = factor[:, None] * accum + jnp.dot(
            weights.astype(jnp.bfloat16), value_h, preferred_element_type=jnp.float32
        )
        return (newmax, total, accum)

    running, total, accum = lax.map(
        per_head, (queries, split_heads(key_piece), split_heads(value_piece)) + start_state
    )
    attended = accum / total[:, :, None]
    logsum = running + jnp.log(total)
    attended_b = merge_heads(attended).astype(jnp.bfloat16)
    hidden = inputs + jnp.dot(attended_b, full_out, preferred_element_type=jnp.float32)
    scale_two = rms_scale(hidden)
    normed_two_b = (hidden * scale_two * full_gtwo.astype(jnp.float32)).astype(jnp.bfloat16)
    upper = jnp.dot(normed_two_b, full_up, preferred_element_type=jnp.float32)
    positive = jnp.maximum(upper, 0.0)
    active_b = (positive * positive).astype(jnp.bfloat16)
    output = hidden + jnp.dot(active_b, full_down, preferred_element_type=jnp.float32)
    back_qkv, back_out, back_up, back_down, back_conv, back_gone, back_gtwo = (
        lax.all_gather(w_qkv, "shard", axis=0, tiled=True),
        lax.all_gather(w_out, "shard", axis=0, tiled=True),
        lax.all_gather(w_up, "shard", axis=0, tiled=True),
        lax.all_gather(w_down, "shard", axis=0, tiled=True),
        lax.all_gather(conv_w, "shard", axis=1, tiled=True),
        lax.all_gather(gain_attn, "shard", axis=0, tiled=True),
        lax.all_gather(gain_ffn, "shard", axis=0, tiled=True),
    )
    incoming = cotangent[0]
    grad_active = jnp.dot(incoming, back_down.T, preferred_element_type=jnp.float32)
    grad_down = jnp.dot(active_b.T, incoming, preferred_element_type=jnp.float32)
    grad_upper_b = (grad_active * 2.0 * positive).astype(jnp.bfloat16)
    grad_up = jnp.dot(normed_two_b.T, grad_upper_b, preferred_element_type=jnp.float32)
    grad_normed_two = jnp.dot(grad_upper_b, back_up.T, preferred_element_type=jnp.float32)
    grad_hidden_norm, grad_gtwo = norm_back(
        hidden, scale_two, back_gtwo.astype(jnp.float32), grad_normed_two
    )
    grad_hidden = incoming.astype(jnp.float32) + grad_hidden_norm
    grad_hidden_b = grad_hidden.astype(jnp.bfloat16)
    grad_out = jnp.dot(attended_b.T, grad_hidden_b, preferred_element_type=jnp.float32)
    grad_attended_b = jnp.dot(grad_hidden_b, back_out.T, preferred_element_type=jnp.float32).astype(
        jnp.bfloat16
    )
    grad_heads = split_heads(grad_attended_b)
    delta_rows = jnp.sum(grad_heads.astype(jnp.float32) * attended, axis=-1)
    key_piece = lax.all_gather(keys_loc, "seq", axis=0, tiled=True)
    value_piece = lax.all_gather(values_loc, "seq", axis=0, tiled=True)
    count = key_piece.shape[0]
    fold_allowed = visible(local_pos, jnp.arange(count, dtype=jnp.int32), prefix_end)

    def per_head(items):
        query_h, grad_h, logsum_h, delta_h, key_h, value_h, grad_q = items
        scores = jnp.dot(query_h, key_h.T, preferred_element_type=jnp.float32) * scale
        probs = jnp.where(fold_allowed, jnp.exp(scores - logsum_h[:, None]), 0.0)
        grad_probs = jnp.dot(grad_h, value_h.T, preferred_element_type=jnp.float32)
        grad_scores = (probs * (grad_probs - delta_h[:, None])).astype(jnp.bfloat16)
        return grad_q + jnp.dot(grad_scores, key_h, preferred_element_type=jnp.float32) * scale

    grad_queries = lax.map(
        per_head,
        (
            queries,
            grad_heads,
            logsum,
            delta_rows,
            split_heads(key_piece),
            split_heads(value_piece),
            jnp.zeros((HEADS, rows, HEAD_DIM), jnp.float32),
        ),
    )
    logsum_all, delta_all = (
        lax.all_gather(logsum, "seq", axis=1, tiled=True),
        lax.all_gather(delta_rows, "seq", axis=1, tiled=True),
    )

    def fold_key_grad(carried, pieces):
        query_piece, grad_piece = pieces
        count = query_piece.shape[0]
        allowed = visible(jnp.arange(count, dtype=jnp.int32), local_pos, prefix_end)

        def per_head(items):
            query_h, grad_h, logsum_h, delta_h, key_h, value_h, grad_k, grad_v = items
            scores = jnp.dot(query_h, key_h.T, preferred_element_type=jnp.float32) * scale
            probs = jnp.where(allowed, jnp.exp(scores - logsum_h[:, None]), 0.0)
            grad_v = grad_v + jnp.dot(
                probs.astype(jnp.bfloat16).T, grad_h, preferred_element_type=jnp.float32
            )
            grad_probs = jnp.dot(grad_h, value_h.T, preferred_element_type=jnp.float32)
            grad_scores = (probs * (grad_probs - delta_h[:, None])).astype(jnp.bfloat16)
            grad_k = (
                grad_k + jnp.dot(grad_scores.T, query_h, preferred_element_type=jnp.float32) * scale
            )
            return (grad_k, grad_v)

        return lax.map(
            per_head,
            (
                split_heads(query_piece),
                split_heads(grad_piece),
                logsum_all,
                delta_all,
                keys_heads,
                values_heads,
            )
            + carried,
        )

    empty_heads = jnp.zeros((HEADS, rows, HEAD_DIM), jnp.float32)
    grad_keys, grad_values = fold_key_grad(
        (empty_heads, empty_heads),
        (
            lax.all_gather(query_rows, "seq", axis=0, tiled=True),
            lax.all_gather(grad_attended_b, "seq", axis=0, tiled=True),
        ),
    )
    grad_mixed_b = jnp.concatenate(
        [merge_heads(grad_queries), merge_heads(grad_keys), merge_heads(grad_values)], 1
    ).astype(jnp.bfloat16)
    after = shifted(grad_mixed_b[:2], "seq", -1)
    grad_extended = jnp.concatenate([grad_mixed_b, after], 0).astype(jnp.float32)
    back_kernel = back_conv.astype(jnp.float32)
    grad_projected_b = (
        back_kernel[0] * grad_extended[:rows]
        + back_kernel[1] * grad_extended[1 : rows + 1]
        + back_kernel[2] * grad_extended[2:]
    ).astype(jnp.bfloat16)
    grad_mixed_f = grad_extended[:rows]
    grad_conv = jnp.stack(
        [
            jnp.sum(grad_mixed_f * extended[2:], axis=0),
            jnp.sum(grad_mixed_f * extended[1 : rows + 1], axis=0),
            jnp.sum(grad_mixed_f * extended[:rows], axis=0),
        ]
    )
    grad_qkv = jnp.dot(normed_b.T, grad_projected_b, preferred_element_type=jnp.float32)
    grad_normed = jnp.dot(grad_projected_b, back_qkv.T, preferred_element_type=jnp.float32)
    grad_input_norm, grad_gone = norm_back(
        inputs, scale_one, back_gone.astype(jnp.float32), grad_normed
    )
    grad_input = (grad_hidden + grad_input_norm).astype(jnp.bfloat16)
    shares = (
        lax.psum_scatter(grad_qkv, "shard", scatter_dimension=0, tiled=True),
        lax.psum_scatter(grad_out, "shard", scatter_dimension=0, tiled=True),
        lax.psum_scatter(grad_up, "shard", scatter_dimension=0, tiled=True),
        lax.psum_scatter(grad_down, "shard", scatter_dimension=0, tiled=True),
        lax.psum_scatter(grad_conv, "shard", scatter_dimension=1, tiled=True),
        lax.psum_scatter(grad_gone, "shard", scatter_dimension=0, tiled=True),
        lax.psum_scatter(grad_gtwo, "shard", scatter_dimension=0, tiled=True),
    )
    totals = lax.psum(
        (shares[0], shares[1], shares[2], shares[3], shares[4], shares[5], shares[6]),
        ("seq", "replica"),
    )
    return (
        output[None].astype(jnp.bfloat16),
        grad_input[None],
        totals[0],
        totals[1],
        totals[2],
        totals[3],
        totals[4],
        totals[5],
        totals[6],
    )


def solution(mesh):
    placed = (
        P(("shard", "replica"), "seq", None),
        P(("shard", "replica")),
        P("shard", None),
        P("shard", None),
        P("shard", None),
        P("shard", None),
        P(None, "shard"),
        P("shard"),
        P("shard"),
        P(("shard", "replica"), "seq", None),
    )
    return jax.shard_map(
        per_device,
        mesh=mesh,
        in_specs=placed,
        out_specs=(
            P(("shard", "replica"), "seq", None),
            P(("shard", "replica"), "seq", None),
            P("shard", None),
            P("shard", None),
            P("shard", None),
            P("shard", None),
            P(None, "shard"),
            P("shard"),
            P("shard"),
        ),
        check_vma=False,
    )
```

profile of v0, /device:TPU:0, one launch (start us, length us, event | category | flops | bytes accessed | tf_op | source)
XLA Modules:
  0.0 1020.8 jit_solution(6217312413911459474)
XLA Ops:
  11.7 8.4 all-reduce.7
  27.8 15.4 %all-gather.10.cloned.1.call-done = bf16[768,2304]{1,0:T(8,128)(2,1)} async-done(((bf16[192,2304]{1,0:T(8,128)(2,1)}), bf16[768,2304]{1,0:T(8,128)(2,1)}) %all-gather.10.cloned.1.call-update) | async-done | bytes 3538960 | tf_op jit(solution)/shard_map/all_gather | solution.py:53
  61.6 59.1 %all-gather.12.cloned.1.call-done = bf16[2048,768]{1,0:T(8,128)(2,1)} async-done(((bf16[512,768]{1,0:T(8,128)(2,1)}), bf16[2048,768]{1,0:T(8,128)(2,1)}) %all-gather.12.cloned.1.call-update) | async-done | bytes 3145744 | tf_op jit(solution)/shard_map/all_gather | solution.py:82
  128.4 56.5 %all-gather.14.cloned.1.call-done = bf16[2048,768]{1,0:T(8,128)(2,1)} async-done(((bf16[512,768]{1,0:T(8,128)(2,1)}), bf16[2048,768]{1,0:T(8,128)(2,1)}) %all-gather.14.cloned.1.call-update) | async-done | bytes 3145744 | tf_op jit(solution)/shard_map/all_gather | solution.py:83
  192.6 103.5 %while.42 = (s32[]{:T(128)}, f32[12,512]{1,0:T(8,128)S(1)}, f32[12,512]{1,0:T(8,128)S(1)}, f32[12,512,64]{1,2,0:T(8,128)}, bf16[12,512,64]{2,1,0:T(8,128)(2,1)},...) while((s32[]{:T(128)}, f32[12,512]{1,0:T(8,128)S(1)}, ...), condition=%wide.region_4.5_spmd.clone.clone, body=%wide.region_1.4_spmd.clone.sunk.clone | while | flops 291538944 | bytes 13940333 | solution.py:100
  300.4 7.1 fusion.119
  307.5 6.6 multiply_convert_fusion.2
  323.5 7.1 fusion.118
  341.7 9.3 fusion.105
  351.0 115.9 %while.43 = (s32[]{:T(128)}, bf16[12,512,64]{1,2,0:T(8,128)(2,1)}, bf16[12,512,64]{2,1,0:T(8,128)(2,1)}, bf16[12,2048,64]{2,1,0:T(8,128)(2,1)}, f32[12,512]{1,0:...) while((s32[]{:T(128)}, bf16[12,512,64]{1,2,0:T(8,128)(2,1)}, ...), condition=%wide.region_9.10_spmd.clone.clone, body=%wide.region_8.9_spmd.clone.sunk.clone | while | flops 412123136 | bytes 10309233 | solution.py:152
  355.1 5.7 fusion.190
  364.6 5.7 fusion.190
  374.1 5.7 fusion.190
  383.6 5.7 fusion.190
  393.1 5.7 fusion.190
  402.6 5.7 fusion.190
  412.0 5.7 fusion.190
  421.6 5.7 fusion.190
  431.2 5.7 fusion.190
  440.7 5.7 fusion.190
  450.1 6.4 fusion.190
  461.0 5.9 fusion.190
  474.1 13.4 %all_gather.60 = f32[12,2048]{1,0:T(8,128)S(1)} all-gather(f32[12,512]{1,0:T(8,128)S(1)} %get-tuple-element.927), channel_id=1, replica_groups=mesh['seq'=4,'shard'=4,'replica'=2] {'seq'}, dimensions={1}, use_global_device_ids=true | all-gather | bytes 122880 | tf_op jit(solution)/shard_map/all_gather | solution.py:166
  487.5 13.3 %all_gather.58 = f32[12,2048]{1,0:T(8,128)S(1)} all-gather(f32[12,512]{1,0:T(8,128)S(1)} %get-tuple-element.928), channel_id=1, replica_groups=mesh['seq'=4,'shard'=4,'replica'=2] {'seq'}, dimensions={1}, use_global_device_ids=true | all-gather | bytes 122880 | tf_op jit(solution)/shard_map/all_gather | solution.py:165
  505.6 148.1 %while.44 = (s32[]{:T(128)}, bf16[12,512,64]{1,2,0:T(8,128)(2,1)}, bf16[12,512,64]{1,2,0:T(8,128)(2,1)}, bf16[12,2048,64]{1,2,0:T(8,128)(2,1)}, bf16[12,512,64]{...) while((s32[]{:T(128)}, bf16[12,512,64]{1,2,0:T(8,128)(2,1)}, ...), condition=%wide.region_11.12_spmd.clone.clone, body=%wide.region_10.11_spmd.clone.sunk.clone | while | flops 547389440 | bytes 14082681 | solution.py:188
  666.6 6.8 multiply_reduce_fusion.2
  682.0 60.6 %reduce-scatter.8.cloned.1.call-done = f32[192,2304]{1,0:T(8,128)} async-done(((f32[768,2304]{1,0:T(8,128)}), f32[192,2304]{1,0:T(8,128)}) %reduce-scatter.8.cloned.1.call-update) | async-done | bytes 1769488 | tf_op jit(solution)/shard_map/reduce_scatter | solution.py:235
  743.2 7.8 fusion.104
  754.4 5.8 all-reduce.6
  763.3 7.5 reduce-scatter.16.cloned.1.call-done
  771.9 39.1 %all-reduce.4 = (f32[3,576]{1,0:T(4,128)}, f32[192]{0:T(256)}, f32[192]{0:T(256)}) all-reduce(f32[3,576]{1,0:T(4,128)S(1)} %copy.101, f32[192]{0:T(256)S(1)} %dynamic-slice.3, f32[192]{0:T(256)S(1)} %dynamic-slice.5), channel_id=1, replica_groups=mesh['seq'=4,'shard'=4,'replica'=2] {'seq','replica'}, use_global_device_ids=true, to_apply=%region_25.26 | all-reduce | flops 2112 | bytes 16896 | tf_op jit(solution)/shard_map/psum | solution.py:243
  811.0 196.2 %all-reduce.10.cloned.1.call-done = (f32[192,2304]{1,0:T(8,128)}, f32[192,768]{1,0:T(8,128)}, f32[192,3072]{1,0:T(8,128)}, f32[768,768]{1,0:T(8,128)}) async-done(((f32[192,2304]{1,0:T(8,128)}, f32[192,768]{1,0:T(8,128)}, f32[192,3072]{1,0:T(8,128)}, f32[768,768]{1,0:T(8,128)}), (f32[192,2304]{1,0:T(8,128)}, f32[192,768]{1,0:T(8,128)}, f32[192,3072]{1,0:T(8,128)}, ...) | async-done | bytes 7077904 | tf_op jit(solution)/shard_map/psum | solution.py:243
  (313 shorter events, 414.1 us)
Async XLA Ops:
  7.2 36.0 %all-gather.10.cloned.1.call-start = ((), (), s32[]{:S(2)}) async-start(), calls=%async_computation.5 | async-start | bytes 4423680 | tf_op jit(solution)/shard_map/all_gather | solution.py:53
  7.9 112.7 %all-gather.12.cloned.1.call-start = ((), (), s32[]{:S(2)}) async-start(), calls=%async_computation.6 | async-start | bytes 3932160 | tf_op jit(solution)/shard_map/all_gather | solution.py:82
  20.1 27.4 %copy-start.17 = (f32[768]{0:T(1024)}, f32[768]{0:T(1024)S(1)}, u32[]{:S(2)}) copy-start(f32[768]{0:T(1024)S(1)} %convert_element_type.91) | copy-start | bytes 9220
  27.8 19.7 %copy-start.19 = (f32[512]{0:T(512)}, f32[512]{0:T(512)S(1)}, u32[]{:S(2)}) copy-start(f32[512]{0:T(512)S(1)} %get-tuple-element.442) | copy-start | bytes 6148
  47.5 4.8 collective-permute-start
  56.2 5.1 copy-start.4
  56.2 128.7 %all-gather.14.cloned.1.call-start = ((), (), s32[]{:S(2)}) async-start(), calls=%async_computation.7 | async-start | bytes 3932160 | tf_op jit(solution)/shard_map/all_gather | solution.py:83
  57.0 240.9 %all-gather.16.cloned.1.call-start = ((), (), s32[]{:S(2)}) async-start(), calls=%async_computation.8 | async-start | bytes 1474560 | tf_op jit(solution)/shard_map/all_gather | solution.py:54
  57.5 242.8 %all-gather.18.cloned.1.call-start = ((), (), s32[]{:S(2)}) async-start(), calls=%async_computation.9 | async-start | bytes 5898240 | tf_op jit(solution)/shard_map/all_gather | solution.py:55
  58.1 249.3 %all-gather.20.cloned.1.call-start = ((), (), s32[]{:S(2)}) async-start(), calls=%async_computation.10 | async-start | bytes 5898240 | tf_op jit(solution)/shard_map/all_gather | solution.py:56
  58.7 410.5 %all-gather.22.cloned.1.call-start = ((), (), s32[]{:S(2)}) async-start(), calls=%async_computation.11 | async-start | bytes 3932160 | tf_op jit(solution)/shard_map/all_gather | solution.py:205
  61.3 439.5 %all-gather.24.cloned.1.call-start = ((), (), s32[]{:S(2)}) async-start(), calls=%async_computation.12 | async-start | bytes 3932160 | tf_op jit(solution)/shard_map/all_gather | solution.py:206
  192.6 105.2 %copy-start.5 = (bf16[1,512,768]{2,1,0:T(8,128)(2,1)S(1)}, bf16[1,512,768]{2,1,0:T(8,128)(2,1)}, u32[]{:S(2)}) copy-start(bf16[1,512,768]{2,1,0:T(8,128)(2,1)} %param.16) | copy-start | bytes 2359300
  297.8 9.6 copy-start.12
  300.4 7.1 copy-start.10
  307.5 6.6 copy-start.9
  320.0 361.9 %reduce-scatter.10.cloned.1.call-start = ((), (), s32[]{:S(2)}) async-start(), calls=%async_computation.14 | async-start | bytes 2949120 | tf_op jit(solution)/shard_map/reduce_scatter | solution.py:236
  323.4 358.5 %reduce-scatter.12.cloned.1.call-start = ((), (), s32[]{:S(2)}) async-start(), calls=%async_computation.15 | async-start | bytes 11796480 | tf_op jit(solution)/shard_map/reduce_scatter | solution.py:237
  330.6 351.3 %reduce-scatter.14.cloned.1.call-start = ((), (), s32[]{:S(2)}) async-start(), calls=%async_computation.16 | async-start | bytes 11796480 | tf_op jit(solution)/shard_map/reduce_scatter | solution.py:238
  351.0 391.6 %reduce-scatter.8.cloned.1.call-start = ((), (), s32[]{:S(2)}) async-start(), calls=%async_computation.13 | async-start | bytes 8847360 | tf_op jit(solution)/shard_map/reduce_scatter | solution.py:235
  659.1 5.5 collective-permute-start.1
  666.6 8.3 copy-start.6
  666.6 8.3 copy-start.18
  666.6 8.2 copy-start.20
  679.9 90.9 %reduce-scatter.16.cloned.1.call-start = ((), (), s32[]{:S(2)}) async-start(), calls=%async_computation.17 | async-start | bytes 1474560
  681.8 325.4 %all-reduce.10.cloned.1.call-start = ((), (), s32[]{:S(2)}) async-start(), calls=%async_computation.18 | async-start | bytes 14155776 | tf_op jit(solution)/shard_map/psum | solution.py:243
  743.2 7.8 copy-start.3
  743.2 7.8 copy-start.7
  743.2 7.8 copy-start.22
  751.0 9.3 copy-start.8
  751.0 9.3 copy-start.21
  1007.2 3.8 copy-start.15
  (8 other events, 16.9 us)
Sparse Core Ops, SparseCore 0:
  9.5 33.5 all-gather.9
  56.4 64.2 all-gather.11
  122.8 62.0 all-gather.13
  186.3 16.0 all-gather.15
  203.8 37.4 all-gather.17
  242.7 37.5 all-gather.19
  281.8 63.4 all-gather.21
  346.9 62.0 all-gather.23
  412.1 31.4 reduce-scatter.9
  446.1 77.9 reduce-scatter.11
  526.6 77.9 reduce-scatter.13
  680.0 62.4 reduce-scatter.7
  745.1 25.6 reduce-scatter.15
  775.1 232.0 all-reduce.9
where the time goes:
time: 1030 us; the launch traced here: 1020 us
  waiting for transfers between devices  404 us (39%)
  matrix products  399 us (39%)
  blocking collectives  85.7 us (8%)
  local copies, waits for them, and re-layouts  61.4 us (6%)
  other arithmetic  46.9 us (5%)
  between operations  16.9 us (2%)
    psum x1, waiting for transfers between devices, per_device(): lax.psum((shares[0], shares[1], shares[2], shares[3], shares[4], shares[5...  196 us
    dot_general x36, matrix products, per_head(): jnp.dot(query_h, key_h.T, preferred_element_type=jnp.float32) * scale  133 us
    dot_general x12, matrix products, per_head(): jnp.dot(grad_scores, key_h, preferred_element_type=jnp.float32) * scale  69 us
    reduce_scatter x1, waiting for transfers between devices, per_device(): lax.psum_scatter(grad_qkv, 'shard', scatter_dimension=0, tiled=True)  60.6 us
    all_gather x1, waiting for transfers between devices, per_device(): key_piece = lax.all_gather(keys_loc, 'seq', axis=0, tiled=True)  59.1 us
    all_gather x1, waiting for transfers between devices, per_device(): value_piece = lax.all_gather(values_loc, 'seq', axis=0, tiled=True)  56.5 us
    dot_general x12, matrix products, per_head(): jnp.dot(grad_scores.T, query_h, preferred_element_type=jnp.float32) * scale  51.6 us
    dot_general x12, matrix products, per_head(): jnp.dot(weights.astype(jnp.bfloat16), value_h, preferred_element_type=jnp...  43.1 us
  transfers between devices with their start and end apart: 16, of which 8 were waited for; matrix products, arithmetic and copies ran while one was open for 48% of the time, Pallas kernels for 0%

commit v1 on v0

v1 whole, which is shorter than its diff:
```python
import functools

import jax
import jax.numpy as jnp
from jax import lax
from jax.experimental import pallas as pl
from jax.experimental.pallas import tpu as pltpu
from jax.sharding import PartitionSpec as P

HEADS = 12
HEAD_DIM=64
NEG=-1e30
F32=jnp.float32
BF=jnp.bfloat16

def nt(a,b):
    return lax.dot_general(a,b,(((1,),(1,)),((),())),preferred_element_type=F32)
def tn(a,b):
    return lax.dot_general(a,b,(((0,),(0,)),((),())),preferred_element_type=F32)

def convolve(proj_ref, conv_ref, wide, heads, parts):
    length, width = proj_ref.shape
    rows = min(512, length)
    wide[0:8] = jnp.zeros((8, width), F32)
    taps = conv_ref[...].astype(F32)
    for c in range(length//rows):
        wide[8+c*rows:8+(c+1)*rows] = proj_ref[c*rows:(c+1)*rows].astype(F32)
    def body(c, _):
        base = pl.multiple_of(c*rows, rows)
        x = wide[pl.ds(base, rows+8)]
        mixed = taps[0:1]*x[8:] + taps[1:2]*x[7:7+rows] + taps[2:3]*x[6:6+rows]
        for p,ref in enumerate(parts):
            for h in range(heads):
                lo = (p*heads+h)*HEAD_DIM
                piece = mixed[:, lo:lo+HEAD_DIM].astype(BF)
                if p == 0:
                    piece = piece * jnp.asarray(HEAD_DIM**-0.5, BF)
                ref[h, pl.ds(base, rows)] = piece
        return 0
    lax.fori_loop(0, length//rows, body, 0)

def mask_t(i, j, rows, prefix):
    kpos = j*rows + lax.broadcasted_iota(jnp.int32, (rows, 1), 0)
    qpos = i*rows + lax.broadcasted_iota(jnp.int32, (1, rows), 1)
    return (kpos <= qpos) | ((kpos < prefix) & (qpos < prefix))

def mask_n(i, j, rows, prefix):
    qpos = i*rows + lax.broadcasted_iota(jnp.int32, (rows, 1), 0)
    kpos = j*rows + lax.broadcasted_iota(jnp.int32, (1, rows), 1)
    return (kpos <= qpos) | ((kpos < prefix) & (qpos < prefix))

def fwd_kernel(prefix_ref, proj_ref, conv_ref, out_ref, lse_ref, wide, qs, ks, vs, m_s, l_s, acc_s, o_s, *, rows):
    heads = qs.shape[0]
    length = proj_ref.shape[0]
    blocks = length//rows
    prefix = prefix_ref[0]
    convolve(proj_ref, conv_ref, wide, heads, (qs, ks, vs))
    def head(h, _):
        def qblock(i, _):
            q = qs[h, pl.ds(pl.multiple_of(i*rows, rows), rows)]
            m_s[...] = jnp.full((1, rows), NEG, F32)
            l_s[...] = jnp.zeros((1, rows), F32)
            acc_s[...] = jnp.zeros((HEAD_DIM, rows), F32)
            def step(j, masked):
                at = pl.ds(pl.multiple_of(j*rows, rows), rows)
                s = nt(ks[h, at], q)
                if masked:
                    s = jnp.where(mask_t(i, j, rows, prefix), s, NEG)
                m_old = m_s[...]
                m_new = jnp.maximum(m_old, jnp.max(s, axis=0, keepdims=True))
                p = jnp.exp(s - m_new)
                a = jnp.exp(m_old - m_new)
                m_s[...] = m_new
                l_s[...] = a*l_s[...] + jnp.sum(p, axis=0, keepdims=True)
                acc_s[...] = a*acc_s[...] + tn(vs[h, at], p.astype(BF))
                return 0
            lax.fori_loop(0, i, lambda j, _: step(j, False), 0)
            lax.fori_loop(i, jnp.maximum(i+1, blocks//2), lambda j, _: step(j, True), 0)
            l = l_s[...]
            o_s[h, pl.ds(pl.multiple_of(i*rows, rows), rows)] = jnp.transpose(acc_s[...]/l).astype(BF)
            lse = m_s[...] + jnp.log(l)
            lse_ref[h, :, pl.ds(pl.multiple_of(i*rows, rows), rows)] = jnp.broadcast_to(lse, (8, rows))
            return 0
        lax.fori_loop(0, blocks, qblock, 0)
        return 0
    lax.fori_loop(0, heads, head, 0)
    def out(c, _):
        at = pl.ds(pl.multiple_of(c*rows, rows), rows)
        out_ref[at] = jnp.concatenate([o_s[h, at] for h in range(heads)], axis=1)
        return 0
    lax.fori_loop(0, blocks, out, 0)

def attention_fwd(prefix, proj, conv, rows=512):
    length, width = proj.shape
    heads = width//(3*HEAD_DIM)
    vm = pl.BlockSpec(memory_space=pltpu.VMEM)
    return pl.pallas_call(
        functools.partial(fwd_kernel, rows=rows),
        out_shape=(jax.ShapeDtypeStruct((length, heads*HEAD_DIM), BF), jax.ShapeDtypeStruct((heads, 8, length), F32)),
        in_specs=[pl.BlockSpec(memory_space=pltpu.SMEM), vm, vm],
        out_specs=(vm, vm),
        scratch_shapes=[pltpu.VMEM((8+length, width), F32)] + [pltpu.VMEM((heads, length, HEAD_DIM), BF)]*3 + [
            pltpu.VMEM((1,rows),F32), pltpu.VMEM((1,rows),F32), pltpu.VMEM((HEAD_DIM,rows),F32), pltpu.VMEM((heads,length,HEAD_DIM),BF)],
        compiler_params=pltpu.CompilerParams(vmem_limit_bytes=60*1024*1024),
        cost_estimate=pl.CostEstimate(flops=4*heads*length*length*HEAD_DIM, bytes_accessed=length*width*2, transcendentals=heads*length*length),
        name="attention_fwd",
    )(prefix, proj, conv)

def bwd_kernel(prefix_ref, proj_ref, conv_ref, do_ref, o_ref, lse_ref, gp_ref, gconv_ref, wide, qs, ks, vs, dos, delta, dq, dk, dv, gq, gk, gv, gwide, *, rows):
    heads = qs.shape[0]
    length, width = proj_ref.shape
    blocks = length//rows
    prefix = prefix_ref[0]
    convolve(proj_ref, conv_ref, wide, heads, (qs, ks, vs))
    def prep(c, _):
        at = pl.ds(pl.multiple_of(c*rows, rows), rows)
        g = do_ref[at]
        prod = g.astype(F32)*o_ref[at].astype(F32)
        for h in range(heads):
            sl = slice(h*HEAD_DIM, (h+1)*HEAD_DIM)
            dos[h, at] = g[:, sl]
            d = jnp.sum(prod[:, sl], axis=1, keepdims=True)
            delta[h, :, at] = jnp.transpose(jnp.broadcast_to(d, (rows, 128)))[0:8]
        return 0
    lax.fori_loop(0, blocks, prep, 0)
    def head(h, _):
        dq[...] = jnp.zeros(dq.shape, F32)
        def kblock(j, _):
            kat = pl.ds(pl.multiple_of(j*rows, rows), rows)
            k = ks[h, kat]; v = vs[h, kat]
            dk[...] = jnp.zeros(dk.shape, F32)
            dv[...] = jnp.zeros(dv.shape, F32)
            def step(i, masked):
                qat = pl.ds(pl.multiple_of(i*rows, rows), rows)
                q = qs[h, qat]; do = dos[h, qat]
                s = nt(k, q)
                p = jnp.exp(s - lse_ref[h, 0:1, qat])
                if masked:
                    p = jnp.where(mask_t(i, j, rows, prefix), p, 0.0)
                dv[...] += jnp.dot(p.astype(BF), do, preferred_element_type=F32)
                dp = nt(v, do)
                ds = (p*(dp - delta[h, 0:1, qat])).astype(BF)
                dk[...] += jnp.dot(ds, q, preferred_element_type=F32)
                dq[qat] += tn(ds, k)
                return 0
            lax.fori_loop(j+1, blocks, lambda i, _: step(i, False), 0)
            lax.fori_loop(jnp.where(j < blocks//2, 0, j), j+1, lambda i, _: step(i, True), 0)
            gk[h, kat] = dk[...].astype(BF)
            gv[h, kat] = dv[...].astype(BF)
            return 0
        lax.fori_loop(0, blocks, kblock, 0)
        def qout(c, _):
            at = pl.ds(pl.multiple_of(c*rows, rows), rows)
            gq[h, at] = (dq[at]*(HEAD_DIM**-0.5)).astype(BF)
            return 0
        lax.fori_loop(0, blocks, qout, 0)
        return 0
    lax.fori_loop(0, heads, head, 0)
    taps = conv_ref[...].astype(F32)
    gwide[length:length+8] = jnp.zeros((8, width), F32)
    def fill(c, _):
        at = pl.ds(pl.multiple_of(c*rows, rows), rows)
        gwide[at] = jnp.concatenate([r[h, at] for r in (gq, gk, gv) for h in range(heads)], axis=1).astype(F32)
        return 0
    lax.fori_loop(0, blocks, fill, 0)
    def out(c, total):
        base = pl.multiple_of(c*rows, rows)
        g = gwide[pl.ds(base, rows+8)]
        x = wide[pl.ds(base, rows+8)]
        g0 = g[:rows]
        gp = taps[0:1]*g0 + taps[1:2]*g[1:rows+1] + taps[2:3]*g[2:rows+2]
        gp_ref[pl.ds(base, rows)] = gp.astype(BF)
        sums = [jnp.sum(g0*x[8-t:8-t+rows], axis=0, keepdims=True) for t in range(3)]
        return tuple(a+b for a, b in zip(total, sums))
    total = lax.fori_loop(0, blocks, out, tuple(jnp.zeros((1, width), F32) for _ in range(3)))
    gconv_ref[...] = jnp.concatenate(total, axis=0)

def attention_bwd(prefix, proj, conv, do, o, lse, rows=512):
    length, width = proj.shape
    heads = width//(3*HEAD_DIM)
    vm = pl.BlockSpec(memory_space=pltpu.VMEM)
    per = lambda dt: pltpu.VMEM((heads, length, HEAD_DIM), dt)
    return pl.pallas_call(
        functools.partial(bwd_kernel, rows=rows),
        out_shape=(jax.ShapeDtypeStruct((length, width), BF), jax.ShapeDtypeStruct((3, width), F32)),
        in_specs=[pl.BlockSpec(memory_space=pltpu.SMEM)] + [vm]*5,
        out_specs=(vm, vm),
        scratch_shapes=[pltpu.VMEM((8+length, width), F32), per(BF), per(BF), per(BF), per(BF), pltpu.VMEM((heads, 8, length), F32),
            pltpu.VMEM((length, HEAD_DIM), F32), pltpu.VMEM((rows, HEAD_DIM), F32), pltpu.VMEM((rows, HEAD_DIM), F32),
            per(BF), per(BF), per(BF), pltpu.VMEM((length+8, width), F32)],
        compiler_params=pltpu.CompilerParams(vmem_limit_bytes=60*1024*1024),
        cost_estimate=pl.CostEstimate(flops=10*heads*length*length*HEAD_DIM, bytes_accessed=length*width*4, transcendentals=heads*length*length),
        name="attention_bwd",
    )(prefix, proj, conv, do, o, lse)


def rms_scale(values):
    return lax.rsqrt(jnp.mean(values * values, axis=-1, keepdims=True) + 1e-06)


def norm_back(values, scale_rows, gain, upstream):
    weighted = upstream * gain
    grad_gain = jnp.sum(upstream * values * scale_rows, axis=0)
    grad_values = scale_rows * weighted - values * scale_rows**3 * jnp.mean(
        weighted * values, axis=-1, keepdims=True
    )
    return (grad_values, grad_gain)


def dot(a, b):
    return jnp.dot(a, b, preferred_element_type=F32)


def per_device(
    tokens, prefix_len, w_qkv, w_out, w_up, w_down, conv_w, gain_attn, gain_ffn, cotangent
):
    blocks = lax.axis_size("seq")
    me = lax.axis_index("seq")
    rows, width = tokens.shape[1:]
    own = HEADS // blocks * HEAD_DIM
    depth = w_qkv.shape[0]

    tokens_all = lax.all_gather(tokens[0], "seq", axis=0, tiled=True)
    columns = lax.dynamic_index_in_dim(w_qkv.reshape(depth, 3, blocks, own), me, 2, False)
    own_qkv = lax.all_gather(columns.reshape(depth, 3 * own), "shard", axis=0, tiled=True)
    small = jnp.concatenate([gain_attn, gain_ffn, conv_w.reshape(-1)])
    small = lax.all_gather(small, "shard", axis=0)
    full_gone = small[:, :depth].reshape(width).astype(F32)
    full_gtwo = small[:, depth : 2 * depth].reshape(width).astype(F32)
    full_conv = small[:, 2 * depth :].reshape(-1, 3, conv_w.shape[1]).transpose(1, 0, 2)
    own_conv = lax.dynamic_index_in_dim(full_conv.reshape(3, 3, blocks, own), me, 2, False)
    own_conv = own_conv.reshape(3, 3 * own)
    full_out = lax.all_gather(w_out, "shard", axis=0, tiled=True)
    full_up = lax.all_gather(w_up, "shard", axis=0, tiled=True)
    full_down = lax.all_gather(w_down, "shard", axis=0, tiled=True)

    whole = tokens_all.astype(F32)
    normed_all = (whole * rms_scale(whole) * full_gone).astype(BF)
    projected = dot(normed_all, own_qkv).astype(BF)
    attended_own, logsum = attention_fwd(prefix_len, projected, own_conv)

    def to_rows(array):
        array = lax.all_to_all(array.reshape(blocks, rows, own), "seq", 0, 0)
        return array.transpose(1, 0, 2).reshape(rows, width)

    def to_heads(array):
        array = array.reshape(rows, blocks, own).transpose(1, 0, 2)
        return lax.all_to_all(array, "seq", 0, 0).reshape(blocks * rows, own)

    inputs = tokens[0].astype(F32)
    scale_one = rms_scale(inputs)
    attended_b = to_rows(attended_own)
    hidden = inputs + dot(attended_b, full_out)
    scale_two = rms_scale(hidden)
    normed_two_b = (hidden * scale_two * full_gtwo).astype(BF)
    positive = jnp.maximum(dot(normed_two_b, full_up), 0.0)
    active_b = (positive * positive).astype(BF)
    output = hidden + dot(active_b, full_down)

    incoming = cotangent[0]
    grad_upper_b = (dot(incoming, full_down.T) * 2.0 * positive).astype(BF)
    grad_normed_two = dot(grad_upper_b, full_up.T)
    grad_hidden_norm, grad_gtwo = norm_back(hidden, scale_two, full_gtwo, grad_normed_two)
    grad_hidden = incoming.astype(F32) + grad_hidden_norm
    grad_hidden_b = grad_hidden.astype(BF)
    grad_attended_b = dot(grad_hidden_b, full_out.T).astype(BF)
    grad_own = to_heads(grad_attended_b)
    grad_down = dot(active_b.T, incoming)
    grad_up = dot(normed_two_b.T, grad_upper_b)
    grad_out = dot(attended_b.T, grad_hidden_b)

    grad_projected, grad_conv = attention_bwd(
        prefix_len, projected, own_conv, grad_own, attended_own, logsum
    )
    grad_normed = lax.psum_scatter(
        dot(grad_projected, own_qkv.T).astype(BF), "seq", scatter_dimension=0, tiled=True
    ).astype(F32)
    grad_qkv = dot(normed_all.T, grad_projected)
    grad_input_norm, grad_gone = norm_back(inputs, scale_one, full_gone, grad_normed)
    grad_input = (grad_hidden + grad_input_norm).astype(BF)

    def shared(grad):
        grad = lax.psum_scatter(grad.astype(BF), "shard", scatter_dimension=0, tiled=True)
        return lax.psum(grad, ("seq", "replica")).astype(F32)

    part = lax.psum_scatter(grad_qkv.astype(BF), "shard", scatter_dimension=0, tiled=True)
    part = lax.psum(part, "replica")
    part = lax.all_gather(part, "seq", axis=0)
    total_qkv = part.reshape(blocks, depth, 3, own).transpose(1, 2, 0, 3).reshape(depth, -1)

    spread = jnp.zeros((3, 3, blocks, own), F32)
    spread = lax.dynamic_update_slice(spread, grad_conv.reshape(3, 3, 1, own), (0, 0, me, 0))
    sums = lax.psum(
        jnp.concatenate([spread.reshape(-1), grad_gone, grad_gtwo]), ("seq", "shard", "replica")
    )
    at = lax.axis_index("shard")
    taps = spread.size
    conv_total = sums[:taps].reshape(3, -1)
    return (
        output[None].astype(BF),
        grad_input[None],
        total_qkv.astype(F32),
        shared(grad_out),
        shared(grad_up),
        shared(grad_down),
        lax.dynamic_slice_in_dim(conv_total, at * conv_w.shape[1], conv_w.shape[1], 1),
        lax.dynamic_slice_in_dim(sums[taps : taps + width], at * depth, depth),
        lax.dynamic_slice_in_dim(sums[taps + width :], at * depth, depth),
    )


def solution(mesh):
    placed = (
        P(("shard", "replica"), "seq", None),
        P(("shard", "replica")),
        P("shard", None),
        P("shard", None),
        P("shard", None),
        P("shard", None),
        P(None, "shard"),
        P("shard"),
        P("shard"),
        P(("shard", "replica"), "seq", None),
    )
    return jax.shard_map(
        per_device,
        mesh=mesh,
        in_specs=placed,
        out_specs=(
            P(("shard", "replica"), "seq", None),
            P(("shard", "replica"), "seq", None),
            P("shard", None),
            P("shard", None),
            P("shard", None),
            P("shard", None),
            P(None, "shard"),
            P("shard"),
            P("shard"),
        ),
        check_vma=False,
    )
```

time: 1030 us -> 664 us (0.64)
  matrix products: 399 us -> 63.1 us
  Pallas kernels: 0 us -> 82.9 us
  waiting for transfers between devices: 404 us -> 324 us
  blocking collectives: 85.7 us -> 125 us
  local copies, waits for them, and re-layouts: 61.4 us -> 25.1 us
  other arithmetic: 46.9 us -> 16.4 us
    dot_general x96 -> x12, matrix products: 399 us -> 63.1 us  [dot(): return jnp.dot(a, b, preferred_element_type=F32)]
    psum x1 -> x2, waiting for transfers between devices: 196 us -> 88.5 us  [the longest x1 72.1 us: shared(): return lax.psum(grad, ('seq', 'replica')).astype(F32)]
    reduce_scatter x4 -> x5, waiting for transfers between devices: 60.7 us -> 155 us  [the longest x3 123 us: shared(): lax.psum_scatter(grad.astype(BF), 'shard', scatter_dimension=0, tiled=True)]
    pallas_call x0 -> x2, Pallas kernels: none -> 82.9 us  [the longest x1 49.8 us: attention_bwd(): pl.pallas_call(functools.partial(bwd_kernel, rows=rows), out_shape=(jax.S...]
    all_gather x8 -> x4, waiting for transfers between devices: 131 us -> 57.6 us  [the longest x1 37.6 us: per_device(): tokens_all = lax.all_gather(tokens[0], 'seq', axis=0, tiled=True)]
    reduce_sum x14 -> x1, other arithmetic: 34.9 us -> 1.96 us  [norm_back(): grad_gain = jnp.sum(upstream * values * scale_rows, axis=0)]
    all_to_all x0 -> x1, blocking collectives: none -> 25.4 us  [to_heads(): return lax.all_to_all(array, 'seq', 0, 0).reshape(blocks * rows, own)]
    unnamed x66 -> x42, local copies, waits for them, and re-layouts: 28 us -> 2.69 us
  transfers between devices with their start and end apart: 16 -> 12, of which waited for: 8 -> 10; matrix products, arithmetic and copies ran while one was open for 48% -> 11% of each run, Pallas kernels for 0% -> 5%
where the time goes in v1:
time: 664 us; the launch traced here: 657 us
  waiting for transfers between devices  324 us (49%)
  blocking collectives  125 us (19%)
  Pallas kernels  82.9 us (12%)
  matrix products  63.1 us (10%)
  local copies, waits for them, and re-layouts  25.1 us (4%)
  other arithmetic  16.4 us (2%)
  between operations  16 us (2%)
    reduce_scatter x3, waiting for transfers between devices, shared(): lax.psum_scatter(grad.astype(BF), 'shard', scatter_dimension=0, tiled=True)  123 us
    psum x1, waiting for transfers between devices, shared(): return lax.psum(grad, ('seq', 'replica')).astype(F32)  72.1 us
    dot_general x12, matrix products, dot(): return jnp.dot(a, b, preferred_element_type=F32)  63.1 us
    pallas_call x1, Pallas kernels, attention_bwd(): pl.pallas_call(functools.partial(bwd_kernel, rows=rows), out_shape=(jax.S...  49.8 us
    psum x1, blocking collectives, per_device(): lax.psum(jnp.concatenate([spread.reshape(-1), grad_gone, grad_gtwo]), ('s...  43.3 us
    all_gather x1, waiting for transfers between devices, per_device(): tokens_all = lax.all_gather(tokens[0], 'seq', axis=0, tiled=True)  37.6 us
    all_gather x1, blocking collectives, per_device(): part = lax.all_gather(part, 'seq', axis=0)  34.6 us
    pallas_call x1, Pallas kernels, attention_fwd(): pl.pallas_call(functools.partial(fwd_kernel, rows=rows), out_shape=(jax.S...  33.1 us
  transfers between devices with their start and end apart: 12, of which 10 were waited for; matrix products, arithmetic and copies ran while one was open for 11% of the time, Pallas kernels for 5%

profile of v1, /device:TPU:0, one launch (start us, length us, event | category | flops | bytes accessed | tf_op | source)
XLA Modules:
  0.0 656.7 jit_solution(5740836608800327714)
XLA Ops:
  15.2 13.2 %all-reduce = bf16[8448]{0:T(1024)(128)(2,1)S(1)} all-reduce(bf16[8448]{0:T(1024)(128)(2,1)S(1)} %dynamic-update-slice), channel_id=3, replica_groups=mesh['seq'=4,'shard'=4,'replica'=2] {'shard'}, use_global_device_ids=true, to_apply=%add | all-reduce | flops 8448 | bytes 33792
  29.6 8.6 %all_gather.30 = bf16[768,576]{1,0:T(8,128)(2,1)S(1)} all-gather(bf16[192,576]{1,0:T(8,128)(2,1)S(1)} %copy.40), channel_id=1, replica_groups=mesh['seq'=4,'shard'=4,'replica'=2] {'shard'}, dimensions={0}, use_global_device_ids=true | all-gather | bytes 1105920 | tf_op jit(solution)/shard_map/all_gather | solution.py:225
  38.2 37.6 %all-gather.13.cloned.1.call-done = bf16[1,2048,768]{2,1,0:T(8,128)(2,1)} async-done(((bf16[1,512,768]{2,1,0:T(8,128)(2,1)}), bf16[1,2048,768]{2,1,0:T(8,128)(2,1)}) %all-gather.13.cloned.1.call-update) | async-done | bytes 3145744 | tf_op jit(solution)/shard_map/all_gather | solution.py:223
  75.8 2.7 fusion
  78.6 4.0 convolution_convert_fusion.3.proj_ref
  82.6 33.1 %attention_fwd.1 = (bf16[2048,192]{1,0:T(8,128)(2,1)}, f32[3,8,2048]{2,1,0:T(8,128)}) custom-call(s32[1]{0:T(128)S(6)} %copy.57.prefix_ref, bf16[2048,576]{1,0:T(8,128)(2,1)} %convolution_convert_fusion.3.proj_ref, bf16[3,576]{1,0:T(4,128)(2,1)} %reshape.131.conv_ref), custom_call_target="tpu_custom_call" | custom-call | flops 3221225472 | bytes 2359296 | tf_op jit(solution)/shard_map/attention_fwd/pallas_call | solution.py:97
  117.9 3.5 all-to-all-start
  121.7 19.8 %all-to-all-done = bf16[4,512,192]{1,2,0:T(8,128)(2,1)S(1)} async-done(((bf16[4,512,192]{1,2,0:T(8,128)(2,1)}), bf16[4,512,192]{1,2,0:T(8,128)(2,1)S(1)}, u32[]{:S(2)}, u32[]{:S(2)}) %all-to-all-start) | async-done | bytes 786464 | tf_op jit(solution)/shard_map/all_to_all | solution.py:243
  141.5 2.3 multiply_reduce_fusion.2
  143.9 7.5 %fusion.22 = f32[512,3072]{1,0:T(8,128)} fusion(bf16[768,3072]{1,0:T(8,128)(2,1)} %all-gather.9.cloned.1.call-done, f32[512,768]{1,0:T(8,128)S(1)} %get-tuple-element.33, f32[768]{0:T(1024)S(1)} %reshape.140, f32[512]{0:T(512)S(1)} %get-tuple-element.31), kind=kOutput, calls=%fused_computation.57 | convolution fusion | flops 2417098752 | bytes 12588032 | tf_op jit(solution)/shard_map/dot_general | solution.py:211
  151.4 20.0 %all-gather.11.cloned.1.call-done = bf16[3072,768]{1,0:T(8,128)(2,1)} async-done(((bf16[768,768]{1,0:T(8,128)(2,1)}), bf16[3072,768]{1,0:T(8,128)(2,1)}) %all-gather.11.cloned.1.call-update) | async-done | bytes 4718608 | tf_op jit(solution)/shard_map/all_gather | solution.py:235
  171.4 7.2 %multiply_convert_fusion = bf16[512,3072]{1,0:T(8,128)(2,1)S(1)} fusion(f32[512,3072]{1,0:T(8,128)} %fusion.22, bf16[3072,768]{1,0:T(8,128)(2,1)} %all-gather.11.cloned.1.call-done, bf16[1,512,768]{2,1,0:T(8,128)(2,1)} %param.19), kind=kOutput, calls=%fused_computation.5 | convolution fusion | flops 2422210560 | bytes 14942208 | tf_op jit(solution)/shard_map/dot_general | solution.py:211
  178.7 2.8 multiply_reduce_fusion
  187.6 25.4 %all_to_all.10 = bf16[4,512,192]{1,2,0:T(8,128)(2,1)} all-to-all(bf16[4,512,192]{1,2,0:T(8,128)(2,1)} %bitcast.56), channel_id=1, replica_groups=mesh['seq'=4,'shard'=4,'replica'=2] {'seq'}, dimensions={0} | all-to-all | bytes 1572864 | tf_op jit(solution)/shard_map/all_to_all | solution.py:248
  215.2 49.8 %attention_bwd.1 = (bf16[2048,576]{1,0:T(8,128)(2,1)}, f32[3,576]{1,0:T(4,128)}) custom-call(s32[1]{0:T(128)S(6)} %copy.57.prefix_ref, bf16[2048,576]{1,0:T(8,128)(2,1)} %convolution_convert_fusion.3.proj_ref, bf16[3,576]{1,0:T(4,128)(2,1)} %reshape.131.conv_ref, bf16[2048,192]{1,0:T(8,128)(2,1)} %bitcast.59, bf16[2048,192]{1,0:T(8,128)(2,1)} %get-tuple-element.13.o_ref, ...), custom_call_target="tpu_custom_call" | custom-call | flops 8053063680 | bytes 4718592 | tf_op jit(solution)/shard_map/attention_bwd/pallas_call | solution.py:183
  265.0 6.4 convolution_convert_fusion.5
  273.4 7.5 %convolution_convert_fusion.1 = bf16[768,3072]{1,0:T(8,128)(2,1)} fusion(bf16[512,3072]{1,0:T(8,128)(2,1)} %copy-done.18, f32[512,768]{1,0:T(8,128)} %copy-done.1, f32[768]{0:T(1024)S(1)} %reshape.140, f32[512]{0:T(512)S(1)} %get-tuple-element.31), kind=kOutput, calls=%fused_computation.8 | convolution fusion | flops 2419458048 | bytes 9442304 | tf_op jit(solution)/shard_map/dot_general | solution.py:211
  282.1 7.6 %convolution_convert_fusion = bf16[3072,768]{1,0:T(8,128)(2,1)} fusion(f32[512,3072]{1,0:T(8,128)} %fusion.22, bf16[1,512,768]{2,1,0:T(8,128)(2,1)S(1)} %copy-done.10), kind=kOutput, calls=%fused_computation.7 | convolution fusion | flops 2422996992 | bytes 11796480 | tf_op jit(solution)/shard_map/dot_general | solution.py:211
  289.7 4.5 reduce-scatter.8.cloned.1.call-done
  294.3 6.1 convolution_convert_fusion.2
  300.7 22.1 %reduce-scatter.10.cloned.1.call-done = bf16[192,768]{1,0:T(8,128)(2,1)} async-done(((bf16[768,768]{1,0:T(8,128)(2,1)}), bf16[192,768]{1,0:T(8,128)(2,1)}) %reduce-scatter.10.cloned.1.call-update) | async-done | bytes 294928 | tf_op jit(solution)/shard_map/reduce_scatter | solution.py:283
  322.8 50.5 %reduce-scatter.12.cloned.1.call-done = bf16[192,3072]{1,0:T(8,128)(2,1)} async-done(((bf16[768,3072]{1,0:T(8,128)(2,1)}), bf16[192,3072]{1,0:T(8,128)(2,1)}) %reduce-scatter.12.cloned.1.call-update) | async-done | bytes 1179664 | tf_op jit(solution)/shard_map/reduce_scatter | solution.py:283
  373.3 50.5 %reduce-scatter.14.cloned.1.call-done = bf16[768,768]{1,0:T(8,128)(2,1)} async-done(((bf16[3072,768]{1,0:T(8,128)(2,1)}), bf16[768,768]{1,0:T(8,128)(2,1)}) %reduce-scatter.14.cloned.1.call-update) | async-done | bytes 1179664 | tf_op jit(solution)/shard_map/reduce_scatter | solution.py:283
  423.9 8.1 %fusion.12 = bf16[1,512,768]{2,1,0:T(8,128)(2,1)} fusion(f32[512,768]{1,0:T(8,128)} %copy-done.1, bf16[3072,768]{1,0:T(8,128)(2,1)} %all-gather.11.cloned.1.call-done, f32[512,3072]{1,0:T(8,128)} %fusion.22), kind=kOutput, calls=%fused_computation.36 | convolution fusion | flops 2421424128 | bytes 13369344 | tf_op jit(solution)/shard_map/dot_general | solution.py:211
  432.9 16.4 %all-reduce.5.cloned.1.call-done = bf16[1,192,576]{2,1,0:T(8,128)(2,1)} async-done(((bf16[1,192,576]{2,1,0:T(8,128)(2,1)}), bf16[1,192,576]{2,1,0:T(8,128)(2,1)}) %all-reduce.5.cloned.1.call-update) | async-done | bytes 221200 | tf_op jit(solution)/shard_map/psum | solution.py:287
  449.3 34.6 %all_gather.35 = bf16[4,192,576]{2,1,0:T(8,128)(2,1)} all-gather(bf16[1,192,576]{2,1,0:T(8,128)(2,1)} %all-reduce.5.cloned.1.call-done), channel_id=1, replica_groups=mesh['seq'=4,'shard'=4,'replica'=2] {'seq'}, dimensions={0}, use_global_device_ids=true | all-gather | bytes 1105920 | tf_op jit(solution)/shard_map/all_gather | solution.py:288
  487.1 4.4 copy.47
  491.4 3.7 reshape.141
  495.1 27.4 %reduce-scatter.6.cloned.1.call-done = bf16[512,768]{1,0:T(8,128)(2,1)} async-done(((bf16[2048,768]{1,0:T(8,128)(2,1)}), bf16[512,768]{1,0:T(8,128)(2,1)}) %reduce-scatter.6.cloned.1.call-update) | async-done | bytes 786448 | tf_op jit(solution)/shard_map/reduce_scatter | solution.py:275
  524.5 43.3 %psum.39 = f32[8448]{0:T(1024)S(1)} all-reduce(f32[8448]{0:T(1024)S(1)} %pad_maximum_fusion), channel_id=1, replica_groups=mesh['seq'=4,'shard'=4,'replica'=2] {'seq','shard','replica'}, use_global_device_ids=true, to_apply=%region_16.17 | all-reduce | flops 8448 | bytes 67584 | tf_op jit(solution)/shard_map/psum | solution.py:293
  571.2 72.1 %all-reduce.7.cloned.1.call-done = (bf16[192,768]{1,0:T(8,128)(2,1)}, bf16[192,3072]{1,0:T(8,128)(2,1)}, bf16[768,768]{1,0:T(8,128)(2,1)}) async-done(((bf16[192,768]{1,0:T(8,128)(2,1)}, bf16[192,3072]{1,0:T(8,128)(2,1)}, bf16[768,768]{1,0:T(8,128)(2,1)}), (bf16[192,768]{1,0:T(8,128)(2,1)}, bf16[192,3072]{1,0:T(8,128)(2,1)}, bf16[768,768]{1,0:T(8,128)(2,1)})) %all-reduce.7.cloned.1.call-update) | async-done | bytes 2654224 | tf_op jit(solution)/shard_map/psum | solution.py:284
  645.2 2.9 convert_element_type.125
  (110 shorter events, 34.9 us)
Async XLA Ops:
  7.2 3.5 copy-start.8
  7.2 68.6 %all-gather.13.cloned.1.call-start = ((), (), s32[]{:S(2)}) async-start(), calls=%async_computation.16 | async-start | bytes 3932160 | tf_op jit(solution)/shard_map/all_gather | solution.py:223
  7.9 113.8 %all-gather.7.cloned.1.call-start = ((), (), s32[]{:S(2)}) async-start(), calls=%async_computation.7 | async-start | bytes 1474560 | tf_op jit(solution)/shard_map/all_gather | solution.py:233
  8.7 135.2 %all-gather.9.cloned.1.call-start = ((), (), s32[]{:S(2)}) async-start(), calls=%async_computation.8 | async-start | bytes 5898240 | tf_op jit(solution)/shard_map/all_gather | solution.py:234
  9.4 162.0 %all-gather.11.cloned.1.call-start = ((), (), s32[]{:S(2)}) async-start(), calls=%async_computation.9 | async-start | bytes 5898240 | tf_op jit(solution)/shard_map/all_gather | solution.py:235
  10.0 3.5 copy-start.13
  10.0 3.6 copy-start.17
  10.0 4.8 copy-start.14
  10.0 4.8 copy-start.15
  38.2 44.4 %copy-start.6 = (bf16[768,576]{1,0:T(8,128)(2,1)}, bf16[768,576]{1,0:T(8,128)(2,1)S(1)}, u32[]{:S(2)}) copy-start(bf16[768,576]{1,0:T(8,128)(2,1)S(1)} %all_gather.30) | copy-start | bytes 2654212
  75.8 2.8 copy-start.4
  115.6 25.9 %copy-start = (bf16[1,512,768]{2,1,0:T(8,128)(2,1)S(1)}, bf16[1,512,768]{2,1,0:T(8,128)(2,1)}, u32[]{:S(2)}) copy-start(bf16[1,512,768]{2,1,0:T(8,128)(2,1)} %param.10) | copy-start | bytes 2359300
  117.9 23.6 %all-to-all-start = ((bf16[4,512,192]{1,2,0:T(8,128)(2,1)}), bf16[4,512,192]{1,2,0:T(8,128)(2,1)S(1)}, u32[]{:S(2)}, u32[]{:S(2)}) async-start(bf16[4,512,192]{1,2,0:T(8,128)(2,1)} %copy.43), calls=%async_computation | async-start | bytes 1572864 | tf_op jit(solution)/shard_map/all_to_all | solution.py:243
  121.4 172.8 %reduce-scatter.8.cloned.1.call-start = ((), (), s32[]{:S(2)}) async-start(), calls=%async_computation.11 | async-start | bytes 1228800 | tf_op jit(solution)/shard_map/reduce_scatter | solution.py:286
  143.9 34.8 %copy-start.1 = (f32[512,768]{1,0:T(8,128)}, f32[512,768]{1,0:T(8,128)S(1)}, u32[]{:S(2)}) copy-start(f32[512,768]{1,0:T(8,128)S(1)} %get-tuple-element.33) | copy-start | bytes 4718596
  171.4 7.3 %copy-start.2 = (bf16[768,3072]{1,0:T(8,128)(2,1)S(1)}, bf16[768,3072]{1,0:T(8,128)(2,1)}, u32[]{:S(2)}) copy-start(bf16[768,3072]{1,0:T(8,128)(2,1)} %all-gather.9.cloned.1.call-done) | copy-start | bytes 14155780
  178.7 2.8 copy-start.18
  178.7 2.9 copy-start.9
  181.6 2.0 copy-start.16
  271.5 51.3 %reduce-scatter.10.cloned.1.call-start = ((), (), s32[]{:S(2)}) async-start(), calls=%async_computation.13 | async-start | bytes 1474560 | tf_op jit(solution)/shard_map/reduce_scatter | solution.py:283
  273.4 100.0 %reduce-scatter.12.cloned.1.call-start = ((), (), s32[]{:S(2)}) async-start(), calls=%async_computation.14 | async-start | bytes 5898240 | tf_op jit(solution)/shard_map/reduce_scatter | solution.py:283
  280.9 1.1 copy-start.10
  280.9 142.9 %reduce-scatter.14.cloned.1.call-start = ((), (), s32[]{:S(2)}) async-start(), calls=%async_computation.15 | async-start | bytes 5898240 | tf_op jit(solution)/shard_map/reduce_scatter | solution.py:283
  289.6 4.6 copy-start.7
  289.7 159.6 %all-reduce.5.cloned.1.call-start = ((), (), s32[]{:S(2)}) async-start(), calls=%async_computation.12 | async-start | bytes 491520 | tf_op jit(solution)/shard_map/psum | solution.py:287
  294.2 228.3 %reduce-scatter.6.cloned.1.call-start = ((), (), s32[]{:S(2)}) async-start(), calls=%async_computation.10 | async-start | bytes 3932160 | tf_op jit(solution)/shard_map/reduce_scatter | solution.py:275
  300.4 343.0 %all-reduce.7.cloned.1.call-start = ((), (), s32[]{:S(2)}) async-start(), calls=%async_computation.17 | async-start | bytes 5308416 | tf_op jit(solution)/shard_map/psum | solution.py:284
  423.9 8.1 %copy-start.12 = (f32[3,576]{1,0:T(4,128)S(1)}, f32[3,576]{1,0:T(4,128)}, u32[]{:S(2)}) copy-start(f32[3,576]{1,0:T(4,128)} %get-tuple-element.16) | copy-start | bytes 20740
  491.4 33.1 %copy-start.11 = (f32[6912]{0:T(1024)S(1)}, f32[6912]{0:T(1024)}, u32[]{:S(2)}) copy-start(f32[6912]{0:T(1024)} %reshape.137) | copy-start | bytes 82948
  522.6 47.3 %copy-start.3 = (bf16[512,768]{1,0:T(8,128)(2,1)S(1)}, bf16[512,768]{1,0:T(8,128)(2,1)}, u32[]{:S(2)}) copy-start(bf16[512,768]{1,0:T(8,128)(2,1)} %reduce-scatter.6.cloned.1.call-done) | copy-start | bytes 2359300
  643.3 4.9 copy-start.5
Sparse Core Ops, SparseCore 0:
  9.6 66.1 all-gather.12
  77.3 16.0 all-gather.6
  95.0 37.5 all-gather.8
  134.0 37.4 all-gather.10
  271.6 22.5 reduce-scatter.7
  297.2 25.5 reduce-scatter.9
  325.3 47.9 reduce-scatter.11
  375.9 47.9 reduce-scatter.13
  426.2 23.0 all-reduce.4
  451.4 71.0 reduce-scatter.5
  526.5 116.7 all-reduce.6

commit v2 on v1

--- a/solution.py
+++ b/solution.py
@@ -194,17 +194,264 @@
     )(prefix, proj, conv, do, o, lse)
 
 
+MESH = pl.DeviceIdType.MESH
+
+
+def reduce_kernel(
+    big_ref, qkv_ref, out_ref, qout_ref, a_buf, b_buf, c_buf, d_buf, qa, qb, qc,
+    a_s, a_r, b_s, b_r, c_s, c_r, d_s, d_r, e_s, e_r, f_s, f_r,
+    *, nx, nz,
+):
+    ny, _, chunks, units = big_ref.shape[:4]
+    half = units // nx
+    piece = half // nz
+    qhalf = qkv_ref.shape[2] // nx
+    z, s, x = lax.axis_index("seq"), lax.axis_index("shard"), lax.axis_index("replica")
+    y, c = s // 2, s % 2
+    core = (z, 2 * y + 1 - c, x)
+
+    def at_y(i):
+        return (y + i) % ny
+
+    def at_x(i):
+        return (x + i) % nx
+
+    def at_z(i):
+        return (z + i) % nz
+
+    def dev_y(i):
+        return (z, 2 * at_y(i) + c, x)
+
+    def dev_x(i):
+        return (z, s, at_x(i))
+
+    def dev_z(i):
+        return (at_z(i), s, x)
+
+    peers = [core] + [dev_y(i) for i in range(1, ny)] + [dev_x(i) for i in range(1, nx)]
+    peers += [dev_z(i) for i in range(1, nz)]
+    barrier = pltpu.get_barrier_semaphore()
+    for peer in peers:
+        pl.semaphore_signal(barrier, inc=1, device_id=peer, device_id_type=MESH)
+    pl.semaphore_wait(barrier, len(peers))
+
+    def copy(src, dst, ss, rs, peer):
+        return pltpu.make_async_remote_copy(
+            src_ref=src, dst_ref=dst, send_sem=ss, recv_sem=rs, device_id=peer, device_id_type=MESH
+        )
+
+    def stage_a(k, _):
+        copy(big_ref.at[:, 1 - c, k], a_buf.at[k], a_s.at[k], a_r.at[k], core).start()
+        return 0
+
+    def wait_a(k):
+        return copy(a_buf.at[k], a_buf.at[k], a_s.at[k], a_r.at[k], core)
+
+    def copy_b(k, i, there):
+        slot = y if there else at_y(i)
+        return copy(a_buf.at[k, at_y(i)], b_buf.at[k, slot], b_s.at[k, at_y(i)], b_r.at[k, slot], dev_y(i))
+
+    def stage_b(k, _):
+        wait_a(k).wait_recv()
+        for i in list(range(1, ny)) + [0]:
+            p = at_y(i)
+            a_buf[k, p] = (a_buf[k, p].astype(F32) + big_ref[p, c, k].astype(F32)).astype(BF)
+            if i:
+                copy_b(k, i, True).start()
+        return 0
+
+    def copy_c(k, i, there):
+        slot = x if there else at_x(i)
+        src = a_buf.at[k, y, pl.ds(at_x(i) * half, half)]
+        return copy(src, c_buf.at[k, slot], c_s.at[k, at_x(i)], c_r.at[k, slot], dev_x(i))
+
+    def stage_c(k):
+        total = a_buf[k, y].astype(F32)
+        for i in range(1, ny):
+            copy_b(k, i, False).wait_recv()
+            total = total + b_buf[k, at_y(i)].astype(F32)
+        a_buf[k, y] = total.astype(BF)
+        for i in range(1, nx):
+            copy_c(k, i, True).start()
+
+    def copy_d(k, i, there):
+        slot = z if there else at_z(i)
+        src = a_buf.at[k, y, pl.ds(x * half + at_z(i) * piece, piece)]
+        return copy(src, d_buf.at[k, slot], d_s.at[k, at_z(i)], d_r.at[k, slot], dev_z(i))
+
+    def stage_d(k):
+        mine = pl.ds(x * half, half)
+        total = a_buf[k, y, mine].astype(F32)
+        for i in range(1, nx):
+            copy_c(k, i, False).wait_recv()
+            total = total + c_buf[k, at_x(i)].astype(F32)
+        a_buf[k, y, mine] = total.astype(BF)
+        for i in range(1, nz):
+            copy_d(k, i, True).start()
+
+    def copy_e(k, i, there):
+        slot = z if there else at_z(i)
+        ref = out_ref.at[k, pl.ds(x * half + slot * piece, piece)]
+        return copy(ref, ref, e_s.at[k, at_z(i)], e_r.at[k, slot], dev_z(i))
+
+    def stage_e(k):
+        mine = pl.ds(x * half + z * piece, piece)
+        total = a_buf[k, y, mine].astype(F32)
+        for i in range(1, nz):
+            copy_d(k, i, False).wait_recv()
+            total = total + d_buf[k, at_z(i)].astype(F32)
+        out_ref[k, mine] = total.astype(BF)
+        for i in range(1, nz):
+            copy_e(k, i, True).start()
+
+    def copy_f(k, i, there):
+        slot = x if there else at_x(i)
+        ref = out_ref.at[k, pl.ds(slot * half, half)]
+        return copy(ref, ref, f_s.at[k, at_x(i)], f_r.at[k, slot], dev_x(i))
+
+    def stage_f(k):
+        for i in range(1, nz):
+            copy_e(k, i, False).wait_recv()
+        for i in range(1, nx):
+            copy_f(k, i, True).start()
+
+    last = chunks
+
+    def q_a():
+        return copy(qkv_ref.at[:, 1 - c], qa, a_s.at[last], a_r.at[last], core)
+
+    def q_b(i, there):
+        slot = y if there else at_y(i)
+        return copy(qa.at[at_y(i)], qb.at[slot], b_s.at[last, at_y(i)], b_r.at[last, slot], dev_y(i))
+
+    def q_c(i, there):
+        slot = x if there else at_x(i)
+        src = qa.at[y, pl.ds(at_x(i) * qhalf, qhalf)]
+        return copy(src, qc.at[slot], c_s.at[last, at_x(i)], c_r.at[last, slot], dev_x(i))
+
+    def q_e(i, there):
+        ref = qout_ref.at[z if there else at_z(i), pl.ds(x * qhalf, qhalf)]
+        return copy(ref, ref, e_s.at[last, at_z(i)], e_r.at[last, z if there else at_z(i)], dev_z(i))
+
+    def q_f(i, there):
+        slot = x if there else at_x(i)
+        ref = qout_ref.at[:, pl.ds(slot * qhalf, qhalf)]
+        return copy(ref, ref, f_s.at[last, at_x(i)], f_r.at[last, slot], dev_x(i))
+
+    q_a().start()
+    lax.fori_loop(0, chunks, stage_a, 0)
+    q_a().wait_recv()
+    for i in list(range(1, ny)) + [0]:
+        p = at_y(i)
+        qa[p] = (qa[p].astype(F32) + qkv_ref[p, c].astype(F32)).astype(BF)
+        if i:
+            q_b(i, True).start()
+    lax.fori_loop(0, chunks, stage_b, 0)
+    total = qa[y].astype(F32)
+    for i in range(1, ny):
+        q_b(i, False).wait_recv()
+        total = total + qb[at_y(i)].astype(F32)
+    qa[y] = total.astype(BF)
+    for i in range(1, nx):
+        q_c(i, True).start()
+
+    def step(t, _):
+        for lag, stage in enumerate((stage_c, stage_d, stage_e, stage_f)):
+            @pl.when((t >= lag) & (t < chunks + lag))
+            def _():
+                stage(t - lag)
+        return 0
+
+    lax.fori_loop(0, 1, step, 0)
+    mine = pl.ds(x * qhalf, qhalf)
+    total = qa[y, mine].astype(F32)
+    for i in range(1, nx):
+        q_c(i, False).wait_recv()
+        total = total + qc[at_x(i)].astype(F32)
+    qout_ref[z, mine] = total.astype(BF)
+    for i in range(1, nz):
+        q_e(i, True).start()
+    lax.fori_loop(1, 3, step, 0)
+    for i in range(1, nz):
+        q_e(i, False).wait_recv()
+    for i in range(1, nx):
+        q_f(i, True).start()
+    lax.fori_loop(3, chunks + 3, step, 0)
+
+    def finish(k, _):
+        for i in range(1, nx):
+            copy_f(k, i, False).wait_recv()
+        wait_a(k).wait_send()
+        for i in range(1, ny):
+            copy_b(k, i, True).wait_send()
+        for i in range(1, nx):
+            copy_c(k, i, True).wait_send()
+            copy_f(k, i, True).wait_send()
+        for i in range(1, nz):
+            copy_d(k, i, True).wait_send()
+            copy_e(k, i, True).wait_send()
+        return 0
+
+    lax.fori_loop(0, chunks, finish, 0)
+    for i in range(1, nx):
+        q_f(i, False).wait_recv()
+    q_a().wait_send()
+    for i in range(1, ny):
+        q_b(i, True).wait_send()
+    for i in range(1, nx):
+        q_c(i, True).wait_send()
+        q_f(i, True).wait_send()
+    for i in range(1, nz):
+        q_e(i, True).wait_send()
+
+
+def reduce_grads(big, qkv, nx, nz):
+    ny, _, chunks, units = big.shape[:4]
+    tail = big.shape[4:]
+    uq = qkv.shape[2]
+    qtail = qkv.shape[3:]
+    half, qhalf = units // nx, uq // nx
+    vm = pl.BlockSpec(memory_space=pltpu.VMEM)
+    sems = []
+    for n in (ny, nx, nz, nz, nx):
+        sems += [pltpu.SemaphoreType.DMA((chunks + 1, n))] * 2
+    return pl.pallas_call(
+        functools.partial(reduce_kernel, nx=nx, nz=nz),
+        out_shape=(
+            jax.ShapeDtypeStruct((chunks, units) + tail, BF),
+            jax.ShapeDtypeStruct((nz, uq) + qtail, BF),
+        ),
+        in_specs=[vm, vm],
+        out_specs=(vm, vm),
+        scratch_shapes=[
+            pltpu.VMEM((chunks, ny, units) + tail, BF),
+            pltpu.VMEM((chunks, ny, units) + tail, BF),
+            pltpu.VMEM((chunks, nx, half) + tail, BF),
+            pltpu.VMEM((chunks, nz, half // nz) + tail, BF),
+            pltpu.VMEM((ny, uq) + qtail, BF),
+            pltpu.VMEM((ny, uq) + qtail, BF),
+            pltpu.VMEM((nx, qhalf) + qtail, BF),
+            pltpu.SemaphoreType.DMA((chunks + 1,)),
+            pltpu.SemaphoreType.DMA((chunks + 1,)),
+        ]
+        + sems,
+        compiler_params=pltpu.CompilerParams(
+            collective_id=1, has_side_effects=True, vmem_limit_bytes=60 * 1024 * 1024
+        ),
+        name="reduce_grads",
+    )(big, qkv)
+
+
 def rms_scale(values):
     return lax.rsqrt(jnp.mean(values * values, axis=-1, keepdims=True) + 1e-06)
 
 
 def norm_back(values, scale_rows, gain, upstream):
     weighted = upstream * gain
-    grad_gain = jnp.sum(upstream * values * scale_rows, axis=0)
     grad_values = scale_rows * weighted - values * scale_rows**3 * jnp.mean(
         weighted * values, axis=-1, keepdims=True
     )
-    return (grad_values, grad_gain)
+    return grad_values
 
 
 def dot(a, b):
@@ -260,15 +507,10 @@
     incoming = cotangent[0]
     grad_upper_b = (dot(incoming, full_down.T) * 2.0 * positive).astype(BF)
     grad_normed_two = dot(grad_upper_b, full_up.T)
-    grad_hidden_norm, grad_gtwo = norm_back(hidden, scale_two, full_gtwo, grad_normed_two)
-    grad_hidden = incoming.astype(F32) + grad_hidden_norm
+    grad_hidden = incoming.astype(F32) + norm_back(hidden, scale_two, full_gtwo, grad_normed_two)
     grad_hidden_b = grad_hidden.astype(BF)
     grad_attended_b = dot(grad_hidden_b, full_out.T).astype(BF)
     grad_own = to_heads(grad_attended_b)
-    grad_down = dot(active_b.T, incoming)
-    grad_up = dot(normed_two_b.T, grad_upper_b)
-    grad_out = dot(attended_b.T, grad_hidden_b)
-
     grad_projected, grad_conv = attention_bwd(
         prefix_len, projected, own_conv, grad_own, attended_own, logsum
     )
@@ -276,36 +518,63 @@
         dot(grad_projected, own_qkv.T).astype(BF), "seq", scatter_dimension=0, tiled=True
     ).astype(F32)
     grad_qkv = dot(normed_all.T, grad_projected)
-    grad_input_norm, grad_gone = norm_back(inputs, scale_one, full_gone, grad_normed)
-    grad_input = (grad_hidden + grad_input_norm).astype(BF)
-
-    def shared(grad):
-        grad = lax.psum_scatter(grad.astype(BF), "shard", scatter_dimension=0, tiled=True)
-        return lax.psum(grad, ("seq", "replica")).astype(F32)
-
-    part = lax.psum_scatter(grad_qkv.astype(BF), "shard", scatter_dimension=0, tiled=True)
-    part = lax.psum(part, "replica")
-    part = lax.all_gather(part, "seq", axis=0)
-    total_qkv = part.reshape(blocks, depth, 3, own).transpose(1, 2, 0, 3).reshape(depth, -1)
-
-    spread = jnp.zeros((3, 3, blocks, own), F32)
-    spread = lax.dynamic_update_slice(spread, grad_conv.reshape(3, 3, 1, own), (0, 0, me, 0))
-    sums = lax.psum(
-        jnp.concatenate([spread.reshape(-1), grad_gone, grad_gtwo]), ("seq", "shard", "replica")
-    )
+    grad_input = (grad_hidden + norm_back(inputs, scale_one, full_gone, grad_normed)).astype(BF)
+
+    shards, copies = lax.axis_size("shard"), lax.axis_size("replica")
+    cut = lambda grad: grad.astype(BF).reshape(shards, -1, 8, width)
+    parts = [
+        cut(dot(normed_two_b.T, grad_upper_b[:, i * width : (i + 1) * width]))
+        for i in range(grad_upper_b.shape[1] // width)
+    ]
+    parts += [cut(dot(active_b.T, incoming)), cut(dot(attended_b.T, grad_hidden_b))]
+    sizes = [part.shape[1] for part in parts]
+    groups = -(-sum(sizes) // (copies * blocks))
+    chunks = -(-groups // max(1, groups // 9))
+    per = max(1, groups // 9) * copies * blocks
+    spare = chunks * per - sum(sizes)
+    if spare:
+        parts.append(jnp.zeros((shards, spare, 8, width), BF))
+    big = jnp.concatenate(parts, axis=1).reshape(shards // 2, 2, chunks, per, 8, width)
+    taps = grad_conv.shape[0]
+    extra = jnp.pad(grad_conv.astype(BF), ((0, 8 - taps), (0, 0)))
+    mine = depth // 8
+    uq = -(-(mine + 1) // copies) * copies
+    qkv = jnp.concatenate(
+        [
+            grad_qkv.astype(BF).reshape(shards, mine, 8, 3 * own),
+            jnp.broadcast_to(extra, (shards, 1, 8, 3 * own)),
+            jnp.zeros((shards, uq - mine - 1, 8, 3 * own), BF),
+        ],
+        axis=1,
+    ).reshape(shards // 2, 2, uq, 8, 3 * own)
+    sums, own_sums = reduce_grads(big, qkv, copies, blocks)
+    sums = sums.reshape(-1, 8, width)
+    cuts = [sum(sizes[:i]) for i in range(len(sizes) + 1)]
+    pieces = [sums[lo:hi].reshape(-1, width).astype(F32) for lo, hi in zip(cuts, cuts[1:])]
+    total_up = jnp.concatenate(pieces[:-2], axis=1)
+
+    def merge(array):
+        return jnp.concatenate(
+            [array[j, :, p * own : (p + 1) * own] for p in range(3) for j in range(blocks)], axis=1
+        ).astype(F32)
+
+    total_qkv = merge(own_sums[:, :mine].reshape(blocks, depth, 3 * own))
+    total_conv = merge(own_sums[:, mine, :taps])
     at = lax.axis_index("shard")
-    taps = spread.size
-    conv_total = sums[:taps].reshape(3, -1)
+
+    def gain_grad(grad, weight, gain):
+        return jnp.sum(grad * weight.astype(F32), axis=1) / gain.astype(F32)
+
     return (
         output[None].astype(BF),
         grad_input[None],
-        total_qkv.astype(F32),
-        shared(grad_out),
-        shared(grad_up),
-        shared(grad_down),
-        lax.dynamic_slice_in_dim(conv_total, at * conv_w.shape[1], conv_w.shape[1], 1),
-        lax.dynamic_slice_in_dim(sums[taps : taps + width], at * depth, depth),
-        lax.dynamic_slice_in_dim(sums[taps + width :], at * depth, depth),
+        total_qkv,
+        pieces[-1],
+        total_up,
+        pieces[-2],
+        lax.dynamic_slice_in_dim(total_conv, at * conv_w.shape[1], conv_w.shape[1], 1),
+        gain_grad(total_qkv, w_qkv, gain_attn),
+        gain_grad(total_up, w_up, gain_ffn),
     )
 
 

time: 664 us -> 449 us (0.68)
  waiting for transfers between devices: 324 us -> 91.8 us
  Pallas kernels: 82.9 us -> 197 us
  blocking collectives: 125 us -> 21.5 us
  matrix products: 63.1 us -> 54.1 us
  local copies, waits for them, and re-layouts: 25.1 us -> 32.1 us
    reduce_scatter x4 -> x0, waiting for transfers between devices: 128 us -> none  [the longest x3 123 us: shared(): lax.psum_scatter(grad.astype(BF), 'shard', scatter_dimension=0, tiled=True)]
    pallas_call x0 -> x1, Pallas kernels: none -> 114 us  [reduce_grads(): pl.pallas_call(functools.partial(reduce_kernel, nx=nx, nz=nz), out_shape=...]
    psum x2 -> x0, waiting for transfers between devices: 88.5 us -> none  [the longest x1 72.1 us: shared(): return lax.psum(grad, ('seq', 'replica')).astype(F32)]
    psum x1 -> x0, blocking collectives: 43.3 us -> none  [per_device(): lax.psum(jnp.concatenate([spread.reshape(-1), grad_gone, grad_gtwo]), ('s...]
    all_gather x1 -> x0, blocking collectives: 34.6 us -> none  [per_device(): part = lax.all_gather(part, 'seq', axis=0)]
    reduce_scatter x1, waiting for transfers between devices: 27.4 us -> 0.01 us  [per_device(): lax.psum_scatter(dot(grad_projected, own_qkv.T).astype(BF), 'seq', scatte...]
    all_to_all x1 -> x0, blocking collectives: 25.4 us -> none  [to_heads(): return lax.all_to_all(array, 'seq', 0, 0).reshape(blocks * rows, own)]
    all_to_all x0 -> x1, waiting for transfers between devices: none -> 13.3 us  [to_heads(): return lax.all_to_all(array, 'seq', 0, 0).reshape(blocks * rows, own)]
  transfers between devices with their start and end apart: 12 -> 7, of which waited for: 10 -> 4; matrix products, arithmetic and copies ran while one was open for 11% -> 18% of each run, Pallas kernels for 5% -> 33%
where the time goes in v2:
time: 449 us; the launch traced here: 442 us
  Pallas kernels  197 us (44%)
  waiting for transfers between devices  91.8 us (20%)
  matrix products  54.1 us (12%)
  local copies, waits for them, and re-layouts  32.1 us (7%)
  blocking collectives  21.5 us (5%)
  other arithmetic  20.4 us (5%)
  between operations  15.8 us (4%)
  starting transfers between devices  8.94 us (2%)
    pallas_call x1, Pallas kernels, reduce_grads(): pl.pallas_call(functools.partial(reduce_kernel, nx=nx, nz=nz), out_shape=...  114 us
    dot_general x15, matrix products, dot(): return jnp.dot(a, b, preferred_element_type=F32)  54.1 us
    pallas_call x1, Pallas kernels, attention_bwd(): pl.pallas_call(functools.partial(bwd_kernel, rows=rows), out_shape=(jax.S...  50 us
    all_gather x1, waiting for transfers between devices, per_device(): tokens_all = lax.all_gather(tokens[0], 'seq', axis=0, tiled=True)  38 us
    pallas_call x1, Pallas kernels, attention_fwd(): pl.pallas_call(functools.partial(fwd_kernel, rows=rows), out_shape=(jax.S...  33.1 us
    all_to_all x1, waiting for transfers between devices, to_rows(): array = lax.all_to_all(array.reshape(blocks, rows, own), 'seq', 0, 0)  20 us
    all_gather x1, waiting for transfers between devices, per_device(): full_down = lax.all_gather(w_down, 'shard', axis=0, tiled=True)  18 us
    all_to_all x1, waiting for transfers between devices, to_heads(): return lax.all_to_all(array, 'seq', 0, 0).reshape(blocks * rows, own)  13.3 us
  transfers between devices with their start and end apart: 7, of which 4 were waited for; matrix products, arithmetic and copies ran while one was open for 18% of the time, Pallas kernels for 33%

profile of v2, /device:TPU:0, one launch (start us, length us, event | category | flops | bytes accessed | tf_op | source)
XLA Modules:
  0.0 441.5 jit_solution(9708758317958538892)
XLA Ops:
  12.4 12.8 %all-reduce.1 = bf16[8448]{0:T(1024)(128)(2,1)S(1)} all-reduce(bf16[8448]{0:T(1024)(128)(2,1)S(1)} %dynamic-update-slice), channel_id=3, replica_groups=mesh['seq'=4,'shard'=4,'replica'=2] {'shard'}, use_global_device_ids=true, to_apply=%add.1 | all-reduce | flops 8448 | bytes 33792
  29.2 8.6 %all_gather.24 = bf16[768,576]{1,0:T(8,128)(2,1)S(1)} all-gather(bf16[192,576]{1,0:T(8,128)(2,1)S(1)} %copy.37), channel_id=1, replica_groups=mesh['seq'=4,'shard'=4,'replica'=2] {'shard'}, dimensions={0}, use_global_device_ids=true | all-gather | bytes 1105920 | tf_op jit(solution)/shard_map/all_gather | solution.py:472
  37.8 38.0 %all-gather.13.cloned.1.call-done = bf16[1,2048,768]{2,1,0:T(8,128)(2,1)} async-done(((bf16[1,512,768]{2,1,0:T(8,128)(2,1)}), bf16[1,2048,768]{2,1,0:T(8,128)(2,1)}) %all-gather.13.cloned.1.call-update) | async-done | bytes 3145744 | tf_op jit(solution)/shard_map/all_gather | solution.py:470
  75.8 2.7 fusion
  78.6 4.0 convolution_convert_fusion.2.proj_ref
  82.6 33.1 %attention_fwd.1 = (bf16[2048,192]{1,0:T(8,128)(2,1)}, f32[3,8,2048]{2,1,0:T(8,128)}) custom-call(s32[1]{0:T(128)S(6)} %copy.52.prefix_ref, bf16[2048,576]{1,0:T(8,128)(2,1)} %convolution_convert_fusion.2.proj_ref, bf16[3,576]{1,0:T(4,128)(2,1)} %reshape.177.conv_ref), custom_call_target="tpu_custom_call" | custom-call | flops 3221225472 | bytes 2359296 | tf_op jit(solution)/shard_map/attention_fwd/pallas_call | solution.py:97
  115.7 2.3 copy.40
  118.0 4.0 all-to-all-start
  122.1 20.0 %all-to-all-done = bf16[4,512,192]{1,2,0:T(8,128)(2,1)S(1)} async-done(((bf16[4,512,192]{1,2,0:T(8,128)(2,1)}), bf16[4,512,192]{1,2,0:T(8,128)(2,1)S(1)}, u32[]{:S(2)}, u32[]{:S(2)}) %all-to-all-start) | async-done | bytes 786464 | tf_op jit(solution)/shard_map/all_to_all | solution.py:490
  142.1 2.3 multiply_reduce_fusion.3
  145.7 7.9 %fusion.23 = f32[512,3072]{1,0:T(8,128)} fusion(bf16[512,768]{1,0:T(8,128)(2,1)} %multiply_convert_fusion.2, bf16[768,3072]{1,0:T(8,128)(2,1)} %all-gather.9.cloned.1.call-done), kind=kOutput, calls=%fused_computation.102 | convolution fusion | flops 2415919104 | bytes 11796480 | tf_op jit(solution)/shard_map/dot_general | solution.py:458
  153.5 18.0 %all-gather.11.cloned.1.call-done = bf16[3072,768]{1,0:T(8,128)(2,1)} async-done(((bf16[768,768]{1,0:T(8,128)(2,1)}), bf16[3072,768]{1,0:T(8,128)(2,1)}) %all-gather.11.cloned.1.call-update) | async-done | bytes 4718608 | tf_op jit(solution)/shard_map/all_gather | solution.py:482
  171.5 7.2 %multiply_convert_fusion = bf16[512,3072]{1,0:T(8,128)(2,1)S(1)} fusion(f32[512,3072]{1,0:T(8,128)} %fusion.23, bf16[3072,768]{1,0:T(8,128)(2,1)} %all-gather.11.cloned.1.call-done, bf16[1,512,768]{2,1,0:T(8,128)(2,1)} %param.19), kind=kOutput, calls=%fused_computation.5 | convolution fusion | flops 2422210560 | bytes 14942208 | tf_op jit(solution)/shard_map/dot_general | solution.py:458
  178.8 2.7 multiply_reduce_fusion.2
  181.5 1.9 subtract_add_fusion
  185.2 2.3 copy.41
  187.5 4.6 %all-to-all-start.1 = ((bf16[4,512,192]{1,2,0:T(8,128)(2,1)}), bf16[4,512,192]{1,2,0:T(8,128)(2,1)}, u32[]{:S(2)}, u32[]{:S(2)}) async-start(bf16[4,512,192]{1,2,0:T(8,128)(2,1)} %bitcast.134), calls=%async_computation.1 | async-start | bytes 1572864 | tf_op jit(solution)/shard_map/all_to_all | solution.py:495
  192.3 2.3 convolution_convert_fusion.7
  199.4 13.3 %all-to-all-done.1 = bf16[4,512,192]{1,2,0:T(8,128)(2,1)} async-done(((bf16[4,512,192]{1,2,0:T(8,128)(2,1)}), bf16[4,512,192]{1,2,0:T(8,128)(2,1)}, u32[]{:S(2)}, u32[]{:S(2)}) %all-to-all-start.1) | async-done | bytes 786464 | tf_op jit(solution)/shard_map/all_to_all | solution.py:495
  212.7 2.2 copy.42
  214.9 50.0 %attention_bwd.1 = (bf16[2048,576]{1,0:T(8,128)(2,1)}, f32[3,576]{1,0:T(4,128)}) custom-call(s32[1]{0:T(128)S(6)} %copy.52.prefix_ref, bf16[2048,576]{1,0:T(8,128)(2,1)} %convolution_convert_fusion.2.proj_ref, bf16[3,576]{1,0:T(4,128)(2,1)} %reshape.177.conv_ref, bf16[2048,192]{1,0:T(8,128)(2,1)} %bitcast.141, bf16[2048,192]{1,0:T(8,128)(2,1)} %get-tuple-element.15.o_ref, ...), custom_call_target="tpu_custom_call" | custom-call | flops 8053063680 | bytes 4718592 | tf_op jit(solution)/shard_map/attention_bwd/pallas_call | solution.py:183
  264.9 6.3 %convolution_convert_fusion.1 = bf16[2048,768]{1,0:T(8,128)(2,1)} fusion(bf16[2048,576]{1,0:T(8,128)(2,1)} %get-tuple-element.17, bf16[768,576]{1,0:T(8,128)(2,1)} %copy-done.13), kind=kOutput, calls=%fused_computation.8 | convolution fusion | flops 1813512192 | bytes 6389760 | tf_op jit(solution)/shard_map/dot_general | solution.py:458
  271.2 2.5 constant_dynamic-update-slice_fusion.4
  274.8 2.2 convolution_convert_fusion.4
  278.2 6.3 %convolution_convert_fusion = bf16[3072,768]{1,0:T(8,128)(2,1)S(1)} fusion(f32[512,3072]{1,0:T(8,128)} %fusion.23, bf16[1,512,768]{2,1,0:T(8,128)(2,1)S(1)} %copy-done.15), kind=kOutput, calls=%fused_computation.7 | convolution fusion | flops 2422996992 | bytes 11796480 | tf_op jit(solution)/shard_map/dot_general | solution.py:458
  284.5 2.5 constant_dynamic-update-slice_fusion.1
  288.9 3.5 fusion.9
  292.5 3.3 convolution_convert_fusion.8
  298.6 113.8 %reduce_grads.1 = (bf16[9,24,8,768]{3,2,1,0:T(8,128)(2,1)}, bf16[4,26,8,576]{3,2,1,0:T(8,128)(2,1)}) custom-call(bf16[2,2,9,24,8,768]{5,4,3,2,1,0:T(8,128)(2,1)} %bitcast.126, bf16[2,2,26,8,576]{4,3,2,1,0:T(8,128)(2,1)} %maximum_maximum_fusion.qkv_ref), custom_call_target="tpu_custom_call" | custom-call | tf_op jit(solution)/shard_map/reduce_grads/pallas_call | solution.py:418
  419.1 2.3 concatenate.28
  422.9 2.2 slice_bitcast_fusion.4
  432.2 2.5 fusion.12
  (127 shorter events, 38.1 us)
Async XLA Ops:
  7.2 3.6 copy-start.23
  7.2 3.5 copy-start.17
  7.2 4.8 %copy-start.20 = (bf16[192]{0:T(256)(128)(2,1)S(1)}, bf16[192]{0:T(256)(128)(2,1)}, u32[]{:S(2)}) copy-start(bf16[192]{0:T(256)(128)(2,1)} %param.18) | copy-start | bytes 1156
  7.2 4.8 %copy-start.18 = (bf16[192]{0:T(256)(128)(2,1)S(1)}, bf16[192]{0:T(256)(128)(2,1)}, u32[]{:S(2)}) copy-start(bf16[192]{0:T(256)(128)(2,1)} %param.17) | copy-start | bytes 1156
  7.2 19.2 %copy-start.5 = (bf16[192,2304]{1,0:T(8,128)(2,1)S(1)}, bf16[192,2304]{1,0:T(8,128)(2,1)}, u32[]{:S(2)}) copy-start(bf16[192,2304]{1,0:T(8,128)(2,1)} %param.12) | copy-start | bytes 2654212
  7.2 68.6 %all-gather.13.cloned.1.call-start = ((), (), s32[]{:S(2)}) async-start(), calls=%async_computation.7 | async-start | bytes 3932160 | tf_op jit(solution)/shard_map/all_gather | solution.py:470
  8.0 114.1 %all-gather.7.cloned.1.call-start = ((), (), s32[]{:S(2)}) async-start(), calls=%async_computation.3 | async-start | bytes 1474560 | tf_op jit(solution)/shard_map/all_gather | solution.py:480
  8.7 136.9 %all-gather.9.cloned.1.call-start = ((), (), s32[]{:S(2)}) async-start(), calls=%async_computation.4 | async-start | bytes 5898240 | tf_op jit(solution)/shard_map/all_gather | solution.py:481
  9.5 162.0 %all-gather.11.cloned.1.call-start = ((), (), s32[]{:S(2)}) async-start(), calls=%async_computation.5 | async-start | bytes 5898240 | tf_op jit(solution)/shard_map/all_gather | solution.py:482
  37.8 44.8 %copy-start.13 = (bf16[768,576]{1,0:T(8,128)(2,1)}, bf16[768,576]{1,0:T(8,128)(2,1)S(1)}, u32[]{:S(2)}) copy-start(bf16[768,576]{1,0:T(8,128)(2,1)S(1)} %all_gather.24) | copy-start | bytes 2654212
  75.8 2.8 copy-start.8
  115.7 26.4 %copy-start = (bf16[1,512,768]{2,1,0:T(8,128)(2,1)S(1)}, bf16[1,512,768]{2,1,0:T(8,128)(2,1)}, u32[]{:S(2)}) copy-start(bf16[1,512,768]{2,1,0:T(8,128)(2,1)} %param.10) | copy-start | bytes 2359300
  118.0 24.1 %all-to-all-start = ((bf16[4,512,192]{1,2,0:T(8,128)(2,1)}), bf16[4,512,192]{1,2,0:T(8,128)(2,1)S(1)}, u32[]{:S(2)}, u32[]{:S(2)}) async-start(bf16[4,512,192]{1,2,0:T(8,128)(2,1)} %copy.40), calls=%async_computation | async-start | bytes 1572864 | tf_op jit(solution)/shard_map/all_to_all | solution.py:490
  144.4 34.4 %copy-start.1 = (f32[512,768]{1,0:T(8,128)}, f32[512,768]{1,0:T(8,128)S(1)}, u32[]{:S(2)}) copy-start(f32[512,768]{1,0:T(8,128)S(1)} %get-tuple-element.63) | copy-start | bytes 4718596
  171.5 7.3 %copy-start.4 = (bf16[768,3072]{1,0:T(8,128)(2,1)S(1)}, bf16[768,3072]{1,0:T(8,128)(2,1)}, u32[]{:S(2)}) copy-start(bf16[768,3072]{1,0:T(8,128)(2,1)} %all-gather.9.cloned.1.call-done) | copy-start | bytes 14155780
  178.8 2.8 copy-start.24
  178.8 2.8 copy-start.14
  187.5 25.2 %all-to-all-start.1 = ((bf16[4,512,192]{1,2,0:T(8,128)(2,1)}), bf16[4,512,192]{1,2,0:T(8,128)(2,1)}, u32[]{:S(2)}, u32[]{:S(2)}) async-start(bf16[4,512,192]{1,2,0:T(8,128)(2,1)} %bitcast.134), calls=%async_computation.1 | async-start | bytes 1572864 | tf_op jit(solution)/shard_map/all_to_all | solution.py:495
  192.1 238.6 %reduce-scatter.2.cloned.1.call-start = ((), (), s32[]{:S(2)}) async-start(), calls=%async_computation.6 | async-start | bytes 3932160 | tf_op jit(solution)/shard_map/reduce_scatter | solution.py:517
  192.3 3.5 copy-start.10
  192.3 3.5 copy-start.25
  271.2 3.6 copy-start.11
  274.8 3.4 copy-start.15
  277.1 11.8 %slice-start = ((s8[6291456]{0:T(1024)(128)(4,1)}), s8[4194304]{0:T(1024)(128)(4,1)S(1)}, s32[]{:S(2)}) async-start(s8[6291456]{0:T(1024)(128)(4,1)} %bitcast.127), calls=%async_computation.8 | async-start | bytes 8388608
  277.1 11.8 %slice-start.2 = ((s8[4718592]{0:T(1024)(128)(4,1)}), s8[4194304]{0:T(1024)(128)(4,1)S(1)}, s32[]{:S(2)}) async-start(s8[4718592]{0:T(1024)(128)(4,1)} %bitcast.143), calls=%async_computation.10 | async-start | bytes 8388608
  278.2 10.7 %slice-start.1 = ((s8[6291456]{0:T(1024)(128)(4,1)}), s8[2097152]{0:T(1024)(128)(4,1)S(1)}, s32[]{:S(2)}) async-start(s8[6291456]{0:T(1024)(128)(4,1)} %bitcast.127), calls=%async_computation.9 | async-start | bytes 4194304
  278.2 10.7 %slice-start.3 = ((s8[4718592]{0:T(1024)(128)(4,1)}), s8[524288]{0:T(1024)(128)(4,1)S(1)}, s32[]{:S(2)}) async-start(s8[4718592]{0:T(1024)(128)(4,1)} %bitcast.143), calls=%async_computation.11 | async-start | bytes 1048576
  288.9 3.5 copy-start.16
  288.9 3.6 copy-start.9
  288.9 3.6 copy-start.26
  421.4 3.8 copy-start.6
  421.4 3.8 copy-start.7
  (6 other events, 11.4 us)
Sparse Core Ops, SparseCore 0:
  9.6 66.1 all-gather.12
  77.4 16.0 all-gather.6
  95.1 37.5 all-gather.8
  134.0 37.4 all-gather.10
  271.3 66.6 reduce-scatter.1

commit v3 on v1

v3 whole, which is shorter than its diff:
```python
import functools

import jax
import jax.numpy as jnp
from jax import lax
from jax.experimental import pallas as pl
from jax.experimental.pallas import tpu as pltpu
from jax.sharding import PartitionSpec as P

HEADS = 12
HEAD_DIM=64
NEG=-1e30
F32=jnp.float32
BF=jnp.bfloat16

def nt(a,b):
    return lax.dot_general(a,b,(((1,),(1,)),((),())),preferred_element_type=F32)
def tn(a,b):
    return lax.dot_general(a,b,(((0,),(0,)),((),())),preferred_element_type=F32)

def convolve(proj_ref, conv_ref, wide, heads, parts):
    length, width = proj_ref.shape
    rows = min(512, length)
    wide[0:8] = jnp.zeros((8, width), F32)
    taps = conv_ref[...].astype(F32)
    for c in range(length//rows):
        wide[8+c*rows:8+(c+1)*rows] = proj_ref[c*rows:(c+1)*rows].astype(F32)
    def body(c, _):
        base = pl.multiple_of(c*rows, rows)
        x = wide[pl.ds(base, rows+8)]
        mixed = taps[0:1]*x[8:] + taps[1:2]*x[7:7+rows] + taps[2:3]*x[6:6+rows]
        for p,ref in enumerate(parts):
            for h in range(heads):
                lo = (p*heads+h)*HEAD_DIM
                piece = mixed[:, lo:lo+HEAD_DIM].astype(BF)
                if p == 0:
                    piece = piece * jnp.asarray(HEAD_DIM**-0.5, BF)
                ref[h, pl.ds(base, rows)] = piece
        return 0
    lax.fori_loop(0, length//rows, body, 0)

def mask_t(i, j, rows, prefix):
    kpos = j*rows + lax.broadcasted_iota(jnp.int32, (rows, 1), 0)
    qpos = i*rows + lax.broadcasted_iota(jnp.int32, (1, rows), 1)
    return (kpos <= qpos) | ((kpos < prefix) & (qpos < prefix))

def mask_n(i, j, rows, prefix):
    qpos = i*rows + lax.broadcasted_iota(jnp.int32, (rows, 1), 0)
    kpos = j*rows + lax.broadcasted_iota(jnp.int32, (1, rows), 1)
    return (kpos <= qpos) | ((kpos < prefix) & (qpos < prefix))

MESH = pl.DeviceIdType.MESH


def remote(src, dst, send, recv, peer):
    return pltpu.make_async_remote_copy(
        src_ref=src, dst_ref=dst, send_sem=send, recv_sem=recv, device_id=peer, device_id_type=MESH
    )


def greet(peers):
    barrier = pltpu.get_barrier_semaphore()
    for peer in peers:
        pl.semaphore_signal(barrier, inc=1, device_id=peer, device_id_type=MESH)
    pl.semaphore_wait(barrier, len(peers))


def fwd_kernel(prefix_ref, proj_ref, conv_ref, own_ref, lse_ref, rows_ref, wide, qs, ks, vs, m_s, l_s, acc_s, o_s, r_s, send, recv):
    heads = qs.shape[0]
    length = proj_ref.shape[0]
    blocks = own_ref.shape[1]
    rows = length // blocks
    prefix = prefix_ref[0]
    z, s_at, x = lax.axis_index("seq"), lax.axis_index("shard"), lax.axis_index("replica")

    def block_copy(h, i, at):
        return remote(o_s.at[h, i], r_s.at[at * heads + h], send.at[h, i], recv.at[h, at], (i, s_at, x))

    greet([((z + i) % blocks, s_at, x) for i in range(1, blocks)])
    convolve(proj_ref, conv_ref, wide, heads, (qs, ks, vs))
    def head(h, _):
        def qblock(i, _):
            q = qs[h, pl.ds(pl.multiple_of(i*rows, rows), rows)]
            m_s[...] = jnp.full((1, rows), NEG, F32)
            l_s[...] = jnp.zeros((1, rows), F32)
            acc_s[...] = jnp.zeros((HEAD_DIM, rows), F32)
            def step(j, masked):
                at = pl.ds(pl.multiple_of(j*rows, rows), rows)
                s = nt(ks[h, at], q)
                if masked:
                    s = jnp.where(mask_t(i, j, rows, prefix), s, NEG)
                m_old = m_s[...]
                m_new = jnp.maximum(m_old, jnp.max(s, axis=0, keepdims=True))
                p = jnp.exp(s - m_new)
                a = jnp.exp(m_old - m_new)
                m_s[...] = m_new
                l_s[...] = a*l_s[...] + jnp.sum(p, axis=0, keepdims=True)
                acc_s[...] = a*acc_s[...] + tn(vs[h, at], p.astype(BF))
                return 0
            lax.fori_loop(0, i, lambda j, _: step(j, False), 0)
            lax.fori_loop(i, jnp.maximum(i+1, blocks//2), lambda j, _: step(j, True), 0)
            l = l_s[...]
            done = (acc_s[...]/l).astype(BF)
            o_s[h, i] = done
            own_ref[h, i] = done
            @pl.when(i != z)
            def _():
                block_copy(h, i, z).start()
            lse = m_s[...] + jnp.log(l)
            lse_ref[h, :, pl.ds(pl.multiple_of(i*rows, rows), rows)] = jnp.broadcast_to(lse, (8, rows))
            return 0
        lax.fori_loop(0, blocks, qblock, 0)
        r_s[z * heads + h] = o_s[h, z]
        return 0
    lax.fori_loop(0, heads, head, 0)
    def finish(h, _):
        for i in range(1, blocks):
            there = (z + i) % blocks
            block_copy(h, there, there).wait_recv()
            block_copy(h, there, z).wait_send()
        return 0
    lax.fori_loop(0, heads, finish, 0)
    rows_ref[...] = r_s[...]

def attention_fwd(prefix, proj, conv, blocks):
    length, width = proj.shape
    heads = width//(3*HEAD_DIM)
    rows = length // blocks
    vm = pl.BlockSpec(memory_space=pltpu.VMEM)
    own = (heads, blocks, HEAD_DIM, rows)
    every = (heads * blocks, HEAD_DIM, rows)
    return pl.pallas_call(
        fwd_kernel,
        out_shape=(jax.ShapeDtypeStruct(own, BF), jax.ShapeDtypeStruct((heads, 8, length), F32), jax.ShapeDtypeStruct(every, BF)),
        in_specs=[pl.BlockSpec(memory_space=pltpu.SMEM), vm, vm],
        out_specs=(vm, vm, vm),
        scratch_shapes=[pltpu.VMEM((8+length, width), F32)] + [pltpu.VMEM((heads, length, HEAD_DIM), BF)]*3 + [
            pltpu.VMEM((1,rows),F32), pltpu.VMEM((1,rows),F32), pltpu.VMEM((HEAD_DIM,rows),F32), pltpu.VMEM(own,BF), pltpu.VMEM(every,BF),
            pltpu.SemaphoreType.DMA((heads, blocks)), pltpu.SemaphoreType.DMA((heads, blocks))],
        compiler_params=pltpu.CompilerParams(vmem_limit_bytes=60*1024*1024, collective_id=2, has_side_effects=True),
        cost_estimate=pl.CostEstimate(flops=4*heads*length*length*HEAD_DIM, bytes_accessed=length*width*2, transcendentals=heads*length*length),
        name="attention_fwd",
    )(prefix, proj, conv)

def split_shard():
    s = lax.axis_index("shard")
    return lax.axis_index("seq"), s // 2, s % 2, lax.axis_index("replica")


class Sums:
    def __init__(self, parts, out_ref, bufs, sems, nz):
        self.parts, self.out = parts, out_ref
        self.a, self.b, self.c, self.d = bufs
        self.sa, self.ra, self.sb, self.rb, self.sc, self.rc, self.sd, self.rd, self.se, self.re, self.sf, self.rf = sems
        self.chunks, self.ny = self.a.shape[:2]
        self.nx = self.c.shape[1]
        self.nz = nz
        self.half = self.c.shape[2]
        self.piece = self.half // nz
        self.me = split_shard()
        z, y, c, x = self.me
        self.core = (z, 2 * y + 1 - c, x)

    def py(self, i):
        return (self.me[1] + i) % self.ny

    def px(self, i):
        return (self.me[3] + i) % self.nx

    def pz(self, i):
        return (self.me[0] + i) % self.nz

    def dy(self, i):
        z, y, c, x = self.me
        return (z, 2 * self.py(i) + c, x)

    def dx(self, i):
        z, y, c, x = self.me
        return (z, 2 * y + c, self.px(i))

    def dz(self, i):
        z, y, c, x = self.me
        return (self.pz(i), 2 * y + c, x)

    def peers(self):
        out = [self.core] + [self.dy(i) for i in range(1, self.ny)]
        out += [self.dx(i) for i in range(1, self.nx)]
        return out + [self.dz(i) for i in range(1, self.nz)]

    def copy_a(self, k, src):
        return remote(src, self.a.at[k], self.sa.at[k], self.ra.at[k], self.core)

    def start(self):
        c = self.me[2]
        for ref, first, count in self.parts:
            for j in range(count):
                src = ref.at[:, 1 - c, j]
                self.copy_a(first + j, src).start()

    def copy_b(self, k, i, there):
        slot = self.me[1] if there else self.py(i)
        return remote(self.a.at[k, self.py(i)], self.b.at[k, slot], self.sb.at[k, self.py(i)], self.rb.at[k, slot], self.dy(i))

    def stage_b(self, k):
        c = self.me[2]
        self.copy_a(k, self.a.at[k]).wait_recv()
        for i in list(range(1, self.ny)) + [0]:
            p = self.py(i)
            for ref, first, count in self.parts:
                @pl.when((k >= first) & (k < first + count))
                def _():
                    j = jnp.clip(k - first, 0, count - 1)
                    self.a[k, p] = (self.a[k, p].astype(F32) + ref[p, c, j].astype(F32)).astype(BF)
            if i:
                self.copy_b(k, i, True).start()

    def copy_c(self, k, i, there):
        slot = self.me[3] if there else self.px(i)
        src = self.a.at[k, self.me[1], pl.ds(self.px(i) * self.half, self.half)]
        return remote(src, self.c.at[k, slot], self.sc.at[k, self.px(i)], self.rc.at[k, slot], self.dx(i))

    def stage_c(self, k):
        y = self.me[1]
        total = self.a[k, y].astype(F32)
        for i in range(1, self.ny):
            self.copy_b(k, i, False).wait_recv()
            total = total + self.b[k, self.py(i)].astype(F32)
        for i in range(1, self.ny):
            self.copy_b(k, i, True).wait_send()
        self.a[k, y] = total.astype(BF)
        for i in range(1, self.nx):
            self.copy_c(k, i, True).start()

    def copy_d(self, k, i, there):
        z, y, c, x = self.me
        slot = z if there else self.pz(i)
        src = self.a.at[k, y, pl.ds(x * self.half + self.pz(i) * self.piece, self.piece)]
        return remote(src, self.d.at[k, slot], self.sd.at[k, self.pz(i)], self.rd.at[k, slot], self.dz(i))

    def stage_d(self, k):
        z, y, c, x = self.me
        mine = pl.ds(x * self.half, self.half)
        total = self.a[k, y, mine].astype(F32)
        for i in range(1, self.nx):
            self.copy_c(k, i, False).wait_recv()
            total = total + self.c[k, self.px(i)].astype(F32)
        for i in range(1, self.nx):
            self.copy_c(k, i, True).wait_send()
        self.a[k, y, mine] = total.astype(BF)
        for i in range(1, self.nz):
            self.copy_d(k, i, True).start()

    def copy_e(self, k, i, there):
        slot = self.me[0] if there else self.pz(i)
        ref = self.out.at[k, pl.ds(self.me[3] * self.half + slot * self.piece, self.piece)]
        return remote(ref, ref, self.se.at[k, self.pz(i)], self.re.at[k, slot], self.dz(i))

    def stage_e(self, k):
        z, y, c, x = self.me
        mine = pl.ds(x * self.half + z * self.piece, self.piece)
        total = self.a[k, y, mine].astype(F32)
        for i in range(1, self.nz):
            self.copy_d(k, i, False).wait_recv()
            total = total + self.d[k, self.pz(i)].astype(F32)
        self.out[k, mine] = total.astype(BF)
        for i in range(1, self.nz):
            self.copy_e(k, i, True).start()

    def copy_f(self, k, i, there):
        slot = self.me[3] if there else self.px(i)
        ref = self.out.at[k, pl.ds(slot * self.half, self.half)]
        return remote(ref, ref, self.sf.at[k, self.px(i)], self.rf.at[k, slot], self.dx(i))

    def stage_f(self, k):
        for i in range(1, self.nz):
            self.copy_e(k, i, False).wait_recv()
        for i in range(1, self.nx):
            self.copy_f(k, i, True).start()

    def step(self, t):
        for lag, stage in enumerate((self.stage_c, self.stage_d, self.stage_e, self.stage_f)):
            @pl.when((t >= lag) & (t < self.chunks + lag))
            def _():
                stage(t - lag)

    def finish(self):
        def body(k, _):
            for i in range(1, self.nx):
                self.copy_f(k, i, False).wait_recv()
            self.copy_a(k, self.a.at[k]).wait_send()
            for i in range(1, self.nx):
                self.copy_f(k, i, True).wait_send()
            for i in range(1, self.nz):
                self.copy_d(k, i, True).wait_send()
                self.copy_e(k, i, True).wait_send()
            return 0

        lax.fori_loop(0, self.chunks, body, 0)

    @staticmethod
    def sems(chunks, ny, nx, nz):
        out = [pltpu.SemaphoreType.DMA((chunks,))] * 2
        for n in (ny, nx, nz, nz, nx):
            out += [pltpu.SemaphoreType.DMA((chunks, n))] * 2
        return out


def bwd_kernel(counts, *refs):
    parts_n = len(counts)
    prefix_ref, proj_ref, conv_ref, do_ref, o_ref, lse_ref = refs[:6]
    part_refs = refs[6:6 + parts_n]
    gp_ref, gconv_ref, sum_ref = refs[6 + parts_n:9 + parts_n]
    wide, qs, ks, vs, dos, delta, dq, dk, dv, gq, gk, gv, gwide, send, recv = refs[9 + parts_n:24 + parts_n]
    bufs = refs[24 + parts_n:28 + parts_n]
    sems = refs[28 + parts_n:]
    heads = qs.shape[0]
    length, width = proj_ref.shape
    blocks = dos.shape[1]
    rows = length//blocks
    prefix = prefix_ref[0]
    parts = []
    first = 0
    for ref, count in zip(part_refs, counts):
        parts.append((ref, first, count))
        first += count
    sums = Sums(parts, sum_ref, bufs, sems, blocks)
    z, y, c, x = sums.me
    greet(sums.peers())
    sums.start()

    def block_copy(h, i, at):
        return remote(do_ref.at[i * heads + h], dos.at[h, at], send.at[h, i], recv.at[h, at], (i, 2 * y + c, x))

    for h in range(heads):
        for i in range(1, blocks):
            block_copy(h, (z + i) % blocks, z).start()
        dos[h, z] = do_ref[z * heads + h]
    convolve(proj_ref, conv_ref, wide, heads, (qs, ks, vs))

    def head(h, _):
        for i in range(1, blocks):
            there = (z + i) % blocks
            block_copy(h, there, there).wait_recv()
        for i in range(blocks):
            prod = dos[h, i].astype(F32) * o_ref[h, i].astype(F32)
            delta[i] = jnp.broadcast_to(jnp.sum(prod, axis=0, keepdims=True), (8, rows))
        dq[...] = jnp.zeros(dq.shape, F32)
        def kblock(j, _):
            t = h*blocks + j
            @pl.when(t < sums.chunks)
            def _():
                sums.stage_b(t)
            turn = (2*t)//3
            @pl.when((turn > 0) & ((2*t)%3 != 2))
            def _():
                sums.step(turn - 1)
            kat = pl.ds(pl.multiple_of(j*rows, rows), rows)
            k = ks[h, kat]; v = vs[h, kat]
            dk[...] = jnp.zeros(dk.shape, F32)
            dv[...] = jnp.zeros(dv.shape, F32)
            def step(i, masked):
                qat = pl.ds(pl.multiple_of(i*rows, rows), rows)
                q = qs[h, qat]; do = dos[h, i]
                s = nt(k, q)
                p = jnp.exp(s - lse_ref[h, 0:1, qat])
                if masked:
                    p = jnp.where(mask_t(i, j, rows, prefix), p, 0.0)
                dv[...] += nt(p.astype(BF), do)
                dp = jnp.dot(v, do, preferred_element_type=F32)
                ds = (p*(dp - delta[i, 0:1])).astype(BF)
                dk[...] += jnp.dot(ds, q, preferred_element_type=F32)
                dq[qat] += tn(ds, k)
                return 0
            lax.fori_loop(j+1, blocks, lambda i, _: step(i, False), 0)
            lax.fori_loop(jnp.where(j < blocks//2, 0, j), j+1, lambda i, _: step(i, True), 0)
            gk[h, kat] = dk[...].astype(BF)
            gv[h, kat] = dv[...].astype(BF)
            return 0
        lax.fori_loop(0, blocks, kblock, 0)
        def qout(c, _):
            at = pl.ds(pl.multiple_of(c*rows, rows), rows)
            gq[h, at] = (dq[at]*(HEAD_DIM**-0.5)).astype(BF)
            return 0
        lax.fori_loop(0, blocks, qout, 0)
        return 0
    lax.fori_loop(0, heads, head, 0)
    steps = heads*blocks
    turns = (2*(steps - 1))//3
    def rest(t, _):
        sums.stage_b(t)
        return 0
    lax.fori_loop(steps, sums.chunks, rest, 0)
    taps = conv_ref[...].astype(F32)
    gwide[length:length+8] = jnp.zeros((8, width), F32)
    def fill(c, _):
        at = pl.ds(pl.multiple_of(c*rows, rows), rows)
        gwide[at] = jnp.concatenate([r[h, at] for r in (gq, gk, gv) for h in range(heads)], axis=1).astype(F32)
        return 0
    lax.fori_loop(0, blocks, fill, 0)
    def out(c, total):
        sums.step(turns + c)
        base = pl.multiple_of(c*rows, rows)
        g = gwide[pl.ds(base, rows+8)]
        x = wide[pl.ds(base, rows+8)]
        g0 = g[:rows]
        gp = taps[0:1]*g0 + taps[1:2]*g[1:rows+1] + taps[2:3]*g[2:rows+2]
        gp_ref[pl.ds(base, rows)] = gp.astype(BF)
        add = [jnp.sum(g0*x[8-t:8-t+rows], axis=0, keepdims=True) for t in range(3)]
        return tuple(a+b for a, b in zip(total, add))
    total = lax.fori_loop(0, blocks, out, tuple(jnp.zeros((1, width), F32) for _ in range(3)))
    gconv_ref[...] = jnp.concatenate(total, axis=0)
    def tail(t, _):
        sums.step(t)
        return 0
    lax.fori_loop(turns + blocks, max(sums.chunks + 3, turns + blocks), tail, 0)
    sums.finish()
    def sent(h, _):
        for i in range(1, blocks):
            block_copy(h, (z + i) % blocks, z).wait_send()
        return 0
    lax.fori_loop(0, heads, sent, 0)

def attention_bwd(prefix, proj, conv, do, o, lse, parts, nx):
    length, width = proj.shape
    heads, blocks = o.shape[:2]
    rows = length // blocks
    counts = tuple(part.shape[2] for part in parts)
    ny, _, _, units = parts[0].shape[:4]
    unit = parts[0].shape[4:]
    chunks = sum(counts)
    half = units // nx
    vm = pl.BlockSpec(memory_space=pltpu.VMEM)
    per = lambda dt: pltpu.VMEM((heads, length, HEAD_DIM), dt)
    return pl.pallas_call(
        functools.partial(bwd_kernel, counts),
        out_shape=(jax.ShapeDtypeStruct((length, width), BF), jax.ShapeDtypeStruct((3, width), F32), jax.ShapeDtypeStruct((chunks, units) + unit, BF)),
        in_specs=[pl.BlockSpec(memory_space=pltpu.SMEM)] + [vm]*(5 + len(parts)),
        out_specs=(vm, vm, vm),
        scratch_shapes=[pltpu.VMEM((8+length, width), F32), per(BF), per(BF), per(BF), pltpu.VMEM(o.shape, BF), pltpu.VMEM((blocks, 8, rows), F32),
            pltpu.VMEM((length, HEAD_DIM), F32), pltpu.VMEM((rows, HEAD_DIM), F32), pltpu.VMEM((rows, HEAD_DIM), F32),
            per(BF), per(BF), per(BF), pltpu.VMEM((length+8, width), F32),
            pltpu.SemaphoreType.DMA((heads, blocks)), pltpu.SemaphoreType.DMA((heads, blocks)),
            pltpu.VMEM((chunks, ny, units) + unit, BF), pltpu.VMEM((chunks, ny, units) + unit, BF),
            pltpu.VMEM((chunks, nx, half) + unit, BF), pltpu.VMEM((chunks, blocks, half // blocks) + unit, BF)]
            + Sums.sems(chunks, ny, nx, blocks),
        compiler_params=pltpu.CompilerParams(vmem_limit_bytes=67043328, collective_id=3, has_side_effects=True),
        cost_estimate=pl.CostEstimate(flops=10*heads*length*length*HEAD_DIM, bytes_accessed=length*width*4, transcendentals=heads*length*length),
        name="attention_bwd",
    )(prefix, proj, conv, do, o, lse, *parts)


def qkv_kernel(part_ref, out_ref, qa, qb, qc, sa, ra, sb, rb, sc, rc, se, re, sf, rf, *, nx, nz):
    ny = part_ref.shape[0]
    half = part_ref.shape[2] // nx
    z, y, c, x = split_shard()
    core = (z, 2 * y + 1 - c, x)

    def py(i):
        return (y + i) % ny

    def px(i):
        return (x + i) % nx

    def pz(i):
        return (z + i) % nz

    def dy(i):
        return (z, 2 * py(i) + c, x)

    def dx(i):
        return (z, 2 * y + c, px(i))

    def dz(i):
        return (pz(i), 2 * y + c, x)

    def to_y(i, there):
        slot = y if there else py(i)
        return remote(qa.at[py(i)], qb.at[slot], sb.at[py(i)], rb.at[slot], dy(i))

    def to_x(i, there):
        slot = x if there else px(i)
        return remote(qa.at[y, pl.ds(px(i) * half, half)], qc.at[slot], sc.at[px(i)], rc.at[slot], dx(i))

    def on_z(i, there):
        slot = z if there else pz(i)
        ref = out_ref.at[slot, pl.ds(x * half, half)]
        return remote(ref, ref, se.at[pz(i)], re.at[slot], dz(i))

    def on_x(i, j, there):
        slot = x if there else px(j)
        ref = out_ref.at[pz(i), pl.ds(slot * half, half)]
        return remote(ref, ref, sf.at[pz(i), px(j)], rf.at[pz(i), slot], dx(j))

    greet([core] + [dy(i) for i in range(1, ny)] + [dx(i) for i in range(1, nx)] + [dz(i) for i in range(1, nz)])
    first = remote(part_ref.at[:, 1 - c], qa, sa.at[0], ra.at[0], core)
    first.start()
    first.wait_recv()
    for i in list(range(1, ny)) + [0]:
        qa[py(i)] = (qa[py(i)].astype(F32) + part_ref[py(i), c].astype(F32)).astype(BF)
        if i:
            to_y(i, True).start()
    total = qa[y].astype(F32)
    for i in range(1, ny):
        to_y(i, False).wait_recv()
        total = total + qb[py(i)].astype(F32)
    qa[y] = total.astype(BF)
    for i in range(1, nx):
        to_x(i, True).start()
    mine = pl.ds(x * half, half)
    total = qa[y, mine].astype(F32)
    for i in range(1, nx):
        to_x(i, False).wait_recv()
        total = total + qc[px(i)].astype(F32)
    out_ref[z, mine] = total.astype(BF)
    for i in range(1, nz):
        on_z(i, True).start()
    for i in range(nz):
        if i:
            on_z(i, False).wait_recv()
        for j in range(1, nx):
            on_x(i, j, True).start()
    for i in range(nz):
        for j in range(1, nx):
            on_x(i, j, False).wait_recv()
            on_x(i, j, True).wait_send()
    first.wait_send()
    for i in range(1, ny):
        to_y(i, True).wait_send()
    for i in range(1, nx):
        to_x(i, True).wait_send()
    for i in range(1, nz):
        on_z(i, True).wait_send()


def reduce_qkv(part, nx, nz):
    ny, _, units = part.shape[:3]
    unit = part.shape[3:]
    vm = pl.BlockSpec(memory_space=pltpu.VMEM)
    dma = pltpu.SemaphoreType.DMA
    return pl.pallas_call(
        functools.partial(qkv_kernel, nx=nx, nz=nz),
        out_shape=jax.ShapeDtypeStruct((nz, units) + unit, BF),
        in_specs=[vm],
        out_specs=vm,
        scratch_shapes=[
            pltpu.VMEM((ny, units) + unit, BF),
            pltpu.VMEM((ny, units) + unit, BF),
            pltpu.VMEM((nx, units // nx) + unit, BF),
        ]
        + [dma((1,))] * 2
        + [dma((ny,))] * 2
        + [dma((nx,))] * 2
        + [dma((nz,))] * 2
        + [dma((nz, nx))] * 2,
        compiler_params=pltpu.CompilerParams(
            collective_id=1, has_side_effects=True, vmem_limit_bytes=60 * 1024 * 1024
        ),
        name="reduce_qkv",
    )(part)


def rms_scale(values):
    return lax.rsqrt(jnp.mean(values * values, axis=-1, keepdims=True) + 1e-06)


def norm_back(values, scale_rows, gain, upstream):
    weighted = upstream * gain
    grad_values = scale_rows * weighted - values * scale_rows**3 * jnp.mean(
        weighted * values, axis=-1, keepdims=True
    )
    return grad_values


def dot(a, b):
    return jnp.dot(a, b, preferred_element_type=F32)


def per_device(
    tokens, prefix_len, w_qkv, w_out, w_up, w_down, conv_w, gain_attn, gain_ffn, cotangent
):
    blocks = lax.axis_size("seq")
    me = lax.axis_index("seq")
    rows, width = tokens.shape[1:]
    own = HEADS // blocks * HEAD_DIM
    depth = w_qkv.shape[0]

    tokens_all = lax.all_gather(tokens[0], "seq", axis=0, tiled=True)
    columns = lax.dynamic_index_in_dim(w_qkv.reshape(depth, 3, blocks, own), me, 2, False)
    own_qkv = lax.all_gather(columns.reshape(depth, 3 * own), "shard", axis=0, tiled=True)
    small = jnp.concatenate([gain_attn, gain_ffn, conv_w.reshape(-1)])
    small = lax.all_gather(small, "shard", axis=0)
    full_gone = small[:, :depth].reshape(width).astype(F32)
    full_gtwo = small[:, depth : 2 * depth].reshape(width).astype(F32)
    full_conv = small[:, 2 * depth :].reshape(-1, 3, conv_w.shape[1]).transpose(1, 0, 2)
    own_conv = lax.dynamic_index_in_dim(full_conv.reshape(3, 3, blocks, own), me, 2, False)
    own_conv = own_conv.reshape(3, 3 * own)
    full_out = lax.all_gather(w_out, "shard", axis=0, tiled=True)
    full_up = lax.all_gather(w_up, "shard", axis=0, tiled=True)
    full_down = lax.all_gather(w_down, "shard", axis=0, tiled=True)

    whole = tokens_all.astype(F32)
    normed_all = (whole * rms_scale(whole) * full_gone).astype(BF)
    projected = dot(normed_all, own_qkv).astype(BF)
    attended_own, logsum, attended = attention_fwd(prefix_len, projected, own_conv, blocks)
    attended = attended.reshape(width, rows)

    inputs = tokens[0].astype(F32)
    scale_one = rms_scale(inputs)
    hidden = inputs + tn(attended, full_out)
    scale_two = rms_scale(hidden)
    normed_two_b = (hidden * scale_two * full_gtwo).astype(BF)
    positive = jnp.maximum(dot(normed_two_b, full_up), 0.0)
    active_b = (positive * positive).astype(BF)
    output = hidden + dot(active_b, full_down)

    incoming = cotangent[0]
    grad_upper_b = (dot(incoming, full_down.T) * 2.0 * positive).astype(BF)
    grad_normed_two = dot(grad_upper_b, full_up.T)
    grad_hidden = incoming.astype(F32) + norm_back(hidden, scale_two, full_gtwo, grad_normed_two)
    grad_hidden_b = grad_hidden.astype(BF)
    grad_attended = nt(full_out, grad_hidden_b).astype(BF)

    shards, copies = lax.axis_size("shard"), lax.axis_size("replica")
    mine = depth // 8

    def cut(grad):
        return grad.astype(BF).reshape(shards // 2, 2, -1, mine, 8, width)

    parts = [
        cut(dot(normed_two_b.T, grad_upper_b[:, i * width : (i + 1) * width]))
        for i in range(grad_upper_b.shape[1] // width)
    ]
    parts += [cut(dot(active_b.T, incoming)), cut(dot(attended, grad_hidden_b))]
    pieces = sum(part.shape[2] for part in parts)
    if mine % (copies * blocks):
        units = -(-pieces * mine // (copies * blocks)) * copies * blocks
        joined = [part.reshape(shards // 2, 2, -1, 8, width) for part in parts]
        joined.append(jnp.zeros((shards // 2, 2, units - pieces * mine, 8, width), BF))
        joined = jnp.concatenate(joined, axis=2)
        parts = [joined.reshape(shards // 2, 2, -1, copies * blocks, 8, width)]

    grad_projected, grad_conv, sums = attention_bwd(
        prefix_len, projected, own_conv, grad_attended.reshape(HEADS, HEAD_DIM, rows),
        attended_own, logsum, parts, copies,
    )
    grad_normed = lax.psum_scatter(
        dot(grad_projected, own_qkv.T).astype(BF), "seq", scatter_dimension=0, tiled=True
    ).astype(F32)
    grad_qkv = dot(normed_all.T, grad_projected)
    grad_input = (grad_hidden + norm_back(inputs, scale_one, full_gone, grad_normed)).astype(BF)

    taps = grad_conv.shape[0]
    extra = jnp.pad(grad_conv.astype(BF), ((0, 8 - taps), (0, 0)))
    uq = -(-(mine + 1) // copies) * copies
    qkv = jnp.concatenate(
        [
            grad_qkv.astype(BF).reshape(shards, mine, 8, 3 * own),
            jnp.broadcast_to(extra, (shards, 1, 8, 3 * own)),
            jnp.zeros((shards, uq - mine - 1, 8, 3 * own), BF),
        ],
        axis=1,
    ).reshape(shards // 2, 2, uq, 8, 3 * own)
    own_sums = reduce_qkv(qkv, copies, blocks)
    sums = sums.reshape(-1, 8, width)[: pieces * mine].reshape(pieces, depth, width)
    ups = w_up.shape[1] // width
    total_up = jnp.concatenate(list(sums[:ups]), axis=1).astype(F32)
    total_down = sums[ups:-1].reshape(-1, width).astype(F32)
    total_out = sums[-1].astype(F32)

    def merge(array):
        return jnp.concatenate(
            [array[j, :, p * own : (p + 1) * own] for p in range(3) for j in range(blocks)], axis=1
        ).astype(F32)

    total_qkv = merge(own_sums[:, :mine].reshape(blocks, depth, 3 * own))
    total_conv = merge(own_sums[:, mine, :taps])
    at = lax.axis_index("shard")

    def gain_grad(grad, weight, gain):
        return jnp.sum(grad * weight.astype(F32), axis=1) / gain.astype(F32)

    return (
        output[None].astype(BF),
        grad_input[None],
        total_qkv,
        total_out,
        total_up,
        total_down,
        lax.dynamic_slice_in_dim(total_conv, at * conv_w.shape[1], conv_w.shape[1], 1),
        gain_grad(total_qkv, w_qkv, gain_attn),
        gain_grad(total_up, w_up, gain_ffn),
    )


def solution(mesh):
    placed = (
        P(("shard", "replica"), "seq", None),
        P(("shard", "replica")),
        P("shard", None),
        P("shard", None),
        P("shard", None),
        P("shard", None),
        P(None, "shard"),
        P("shard"),
        P("shard"),
        P(("shard", "replica"), "seq", None),
    )
    return jax.shard_map(
        per_device,
        mesh=mesh,
        in_specs=placed,
        out_specs=(
            P(("shard", "replica"), "seq", None),
            P(("shard", "replica"), "seq", None),
            P("shard", None),
            P("shard", None),
            P("shard", None),
            P("shard", None),
            P(None, "shard"),
            P("shard"),
            P("shard"),
        ),
        check_vma=False,
    )
```

time: 664 us -> 407 us (0.61)
  the two profiles are of different devices: /device:TPU:0 before, /device:TPU:8 now
where the time goes in v3:
time: 407 us; the launch traced here: 404 us
  Pallas kernels  198 us (49%)
  waiting for transfers between devices  81.6 us (20%)
  matrix products  54 us (13%)
  blocking collectives  20.5 us (5%)
  other arithmetic  17.2 us (4%)
  between operations  15.9 us (4%)
  local copies, waits for them, and re-layouts  15.8 us (4%)
    pallas_call x1, Pallas kernels, attention_bwd(): pl.pallas_call(functools.partial(bwd_kernel, counts), out_shape=(jax.Shap...  105 us
    pallas_call x1, Pallas kernels, reduce_qkv(): pl.pallas_call(functools.partial(qkv_kernel, nx=nx, nz=nz), out_shape=jax...  56.3 us
    dot_general x13, matrix products, dot(): return jnp.dot(a, b, preferred_element_type=F32)  50.7 us
    pallas_call x1, Pallas kernels, attention_fwd(): pl.pallas_call(fwd_kernel, out_shape=(jax.ShapeDtypeStruct(own, BF), jax....  37.4 us
    all_gather x1, waiting for transfers between devices, per_device(): tokens_all = lax.all_gather(tokens[0], 'seq', axis=0, tiled=True)  35 us
    all_gather x1, waiting for transfers between devices, per_device(): full_down = lax.all_gather(w_down, 'shard', axis=0, tiled=True)  32.2 us
    all_gather x1, waiting for transfers between devices, per_device(): full_up = lax.all_gather(w_up, 'shard', axis=0, tiled=True)  11.9 us
    unnamed x1, blocking collectives  11.8 us
  transfers between devices with their start and end apart: 5, of which 3 were waited for; matrix products, arithmetic and copies ran while one was open for 12% of the time, Pallas kernels for 23%

profile of v3, /device:TPU:8, one launch (start us, length us, event | category | flops | bytes accessed | tf_op | source)
XLA Modules:
  0.0 403.8 jit_solution(2491623885269854151)
XLA Ops:
  15.2 11.8 %all-reduce.1 = bf16[8448]{0:T(1024)(128)(2,1)S(1)} all-reduce(bf16[8448]{0:T(1024)(128)(2,1)S(1)} %dynamic-update-slice), channel_id=3, replica_groups=mesh['seq'=4,'shard'=4,'replica'=2] {'shard'}, use_global_device_ids=true, to_apply=%add.1 | all-reduce | flops 8448 | bytes 33792
  28.3 8.8 %all_gather.24 = bf16[768,576]{1,0:T(8,128)(2,1)S(1)} all-gather(bf16[192,576]{1,0:T(8,128)(2,1)S(1)} %copy.33), channel_id=1, replica_groups=mesh['seq'=4,'shard'=4,'replica'=2] {'shard'}, dimensions={0}, use_global_device_ids=true | all-gather | bytes 1105920 | tf_op jit(solution)/shard_map/all_gather | solution.py:589
  37.0 35.0 %all-gather.13.cloned.1.call-done = bf16[1,2048,768]{2,1,0:T(8,128)(2,1)} async-done(((bf16[1,512,768]{2,1,0:T(8,128)(2,1)}), bf16[1,2048,768]{2,1,0:T(8,128)(2,1)}) %all-gather.13.cloned.1.call-update) | async-done | bytes 3145744 | tf_op jit(solution)/shard_map/all_gather | solution.py:587
  72.0 2.7 fusion
  74.9 4.1 %convolution_convert_fusion.2.proj_ref.refs_1_ = bf16[2048,576]{1,0:T(8,128)(2,1)} fusion(bf16[768,576]{1,0:T(8,128)(2,1)S(1)} %all_gather.24, bf16[1,2048,768]{2,1,0:T(8,128)(2,1)S(1)} %copy-done.12, f32[768]{0:T(1024)S(1)} %reshape.165, f32[2048]{0:T(1024)S(1)} %add_rsqrt_fusion), kind=kOutput, calls=%fused_computation.9 | convolution fusion | flops 1819410432 | bytes 6401024 | tf_op jit(solution)/shard_map/dot_general | solution.py:575
  78.9 37.4 %attention_fwd.1 = (bf16[3,4,64,512]{3,2,1,0:T(8,128)(2,1)}, f32[3,8,2048]{2,1,0:T(8,128)}, bf16[12,64,512]{2,1,0:T(8,128)(2,1)}) custom-call(s32[1]{0:T(128)S(6)} %copy.41.prefix_ref.refs_0_, bf16[2048,576]{1,0:T(8,128)(2,1)} %convolution_convert_fusion.2.proj_ref.refs_1_, bf16[3,576]{1,0:T(4,128)(2,1)} %reshape.155.conv_ref.refs_2_), custom_call_target="tpu_custom_call" | custom-call | flops 3221225472 | bytes 2359296 | tf_op jit(solution)/shard_map/attention_fwd/pallas_call | solution.py:132
  116.4 2.4 multiply_reduce_fusion.3
  119.1 11.9 %all-gather.9.cloned.1.call-done = bf16[768,3072]{1,0:T(8,128)(2,1)} async-done(((bf16[192,3072]{1,0:T(8,128)(2,1)}), bf16[768,3072]{1,0:T(8,128)(2,1)}) %all-gather.9.cloned.1.call-update) | async-done | bytes 4718608 | tf_op jit(solution)/shard_map/all_gather | solution.py:598
  131.0 6.8 %fusion.24 = f32[512,3072]{1,0:T(8,128)} fusion(bf16[512,768]{1,0:T(8,128)(2,1)S(1)} %multiply_convert_fusion.2, bf16[768,3072]{1,0:T(8,128)(2,1)} %all-gather.9.cloned.1.call-done), kind=kOutput, calls=%fused_computation.97 | convolution fusion | flops 2415919104 | bytes 11796480 | tf_op jit(solution)/shard_map/dot_general | solution.py:575
  137.8 32.2 %all-gather.11.cloned.1.call-done = bf16[3072,768]{1,0:T(8,128)(2,1)} async-done(((bf16[768,768]{1,0:T(8,128)(2,1)}), bf16[3072,768]{1,0:T(8,128)(2,1)}) %all-gather.11.cloned.1.call-update) | async-done | bytes 4718608 | tf_op jit(solution)/shard_map/all_gather | solution.py:599
  170.0 6.2 %multiply_convert_fusion = bf16[512,3072]{1,0:T(8,128)(2,1)S(1)} fusion(f32[512,3072]{1,0:T(8,128)} %fusion.24, bf16[3072,768]{1,0:T(8,128)(2,1)} %all-gather.11.cloned.1.call-done, bf16[1,512,768]{2,1,0:T(8,128)(2,1)S(1)} %copy-done.16), kind=kOutput, calls=%fused_computation.5 | convolution fusion | flops 2422210560 | bytes 14942208 | tf_op jit(solution)/shard_map/dot_general | solution.py:575
  176.1 1.8 convolution_convert_fusion.7
  178.0 1.8 convolution_convert_fusion.6
  179.8 1.8 convolution_convert_fusion.5
  181.6 1.8 convolution_convert_fusion.4
  183.5 4.5 %convolution_convert_fusion = bf16[3072,768]{1,0:T(8,128)(2,1)} fusion(f32[512,3072]{1,0:T(8,128)S(1)} %copy-done.4, bf16[1,512,768]{2,1,0:T(8,128)(2,1)S(1)} %copy-done.16), kind=kOutput, calls=%fused_computation.7 | convolution fusion | flops 2422996992 | bytes 11796480 | tf_op jit(solution)/shard_map/dot_general | solution.py:575
  188.1 2.7 multiply_reduce_fusion.2
  192.0 1.8 convolution_convert_fusion.3
  196.1 104.7 %attention_bwd.1 = (bf16[2048,576]{1,0:T(8,128)(2,1)}, f32[3,576]{1,0:T(4,128)}, bf16[9,24,8,768]{3,2,1,0:T(8,128)(2,1)}) custom-call(s32[1]{0:T(128)S(6)} %copy.41.prefix_ref.refs_0_, bf16[2048,576]{1,0:T(8,128)(2,1)} %convolution_convert_fusion.2.proj_ref.refs_1_, bf16[3,576]{1,0:T(4,128)(2,1)} %reshape.155.conv_ref.refs_2_, ...), custom_call_target="tpu_custom_call" | custom-call | flops 8053063680 | bytes 4718592 | tf_op jit(solution)/shard_map/attention_bwd/pallas_call | solution.py:434
  300.8 6.4 %convolution_convert_fusion.1 = bf16[2048,768]{1,0:T(8,128)(2,1)} fusion(bf16[2048,576]{1,0:T(8,128)(2,1)} %get-tuple-element.18, bf16[768,576]{1,0:T(8,128)(2,1)} %copy-done.14), kind=kOutput, calls=%fused_computation.8 | convolution fusion | flops 1813512192 | bytes 6389760 | tf_op jit(solution)/shard_map/dot_general | solution.py:575
  309.1 4.9 %convolution_convert_fusion.8 = bf16[768,576]{0,1:T(8,128)(2,1)} fusion(bf16[2048,576]{1,0:T(8,128)(2,1)} %get-tuple-element.18, bf16[1,2048,768]{2,1,0:T(8,128)(2,1)S(1)} %copy-done.13, f32[768]{0:T(1024)S(1)} %copy-done.18, f32[2048]{0:T(1024)S(1)} %copy-done.21), kind=kOutput, calls=%fused_computation.34 | convolution fusion | flops 1818673152 | bytes 6401024 | tf_op jit(solution)/shard_map/dot_general | solution.py:575
  314.0 1.5 copy.37
  316.7 56.3 %reduce_qkv.1 = bf16[4,26,8,576]{3,2,1,0:T(8,128)(2,1)} custom-call(bf16[2,2,26,8,576]{4,3,2,1,0:T(8,128)(2,1)} %maximum_maximum_fusion.part_ref), custom_call_target="tpu_custom_call" | custom-call | tf_op jit(solution)/shard_map/reduce_qkv/pallas_call | solution.py:540
  373.1 1.4 slice.138
  375.7 2.2 concatenate.21
  378.9 2.3 slice_bitcast_fusion.4
  381.2 1.4 multiply_reduce_fusion.1
  382.7 1.7 multiply_reduce_fusion
  385.0 1.7 bitcast_convert_fusion
  386.7 5.9 %fusion.9 = bf16[1,512,768]{2,1,0:T(8,128)(2,1)} fusion(f32[512,768]{1,0:T(8,128)S(1)} %copy-done.6, bf16[3072,768]{1,0:T(8,128)(2,1)} %all-gather.11.cloned.1.call-done, f32[512,3072]{1,0:T(8,128)S(1)} %bitcast.122), kind=kOutput, calls=%fused_computation.36 | convolution fusion | flops 2421424128 | bytes 13369344 | tf_op jit(solution)/shard_map/dot_general | solution.py:575
  392.6 1.7 fusion.3
  394.3 2.5 fusion.13
  (119 shorter events, 17.5 us)
Async XLA Ops:
  7.2 3.6 copy-start.9
  7.2 64.8 %all-gather.13.cloned.1.call-start = ((), (), s32[]{:S(2)}) async-start(), calls=%async_computation.5 | async-start | bytes 3932160 | tf_op jit(solution)/shard_map/all_gather | solution.py:587
  7.9 108.5 %all-gather.7.cloned.1.call-start = ((), (), s32[]{:S(2)}) async-start(), calls=%async_computation.1 | async-start | bytes 1474560 | tf_op jit(solution)/shard_map/all_gather | solution.py:597
  8.7 122.3 %all-gather.9.cloned.1.call-start = ((), (), s32[]{:S(2)}) async-start(), calls=%async_computation.2 | async-start | bytes 5898240 | tf_op jit(solution)/shard_map/all_gather | solution.py:598
  9.4 160.6 %all-gather.11.cloned.1.call-start = ((), (), s32[]{:S(2)}) async-start(), calls=%async_computation.3 | async-start | bytes 5898240 | tf_op jit(solution)/shard_map/all_gather | solution.py:599
  10.0 3.5 copy-start.22
  10.0 3.6 copy-start.28
  10.0 4.8 %copy-start.23 = (bf16[192]{0:T(256)(128)(2,1)S(1)}, bf16[192]{0:T(256)(128)(2,1)}, u32[]{:S(2)}) copy-start(bf16[192]{0:T(256)(128)(2,1)} %param.17) | copy-start | bytes 1156
  10.0 4.8 %copy-start.25 = (bf16[192]{0:T(256)(128)(2,1)S(1)}, bf16[192]{0:T(256)(128)(2,1)}, u32[]{:S(2)}) copy-start(bf16[192]{0:T(256)(128)(2,1)} %param.18) | copy-start | bytes 1156
  10.0 382.6 %reduce-scatter.2.cloned.1.call-start = ((), (), s32[]{:S(2)}) async-start(), calls=%async_computation.4 | async-start | bytes 3932160 | tf_op jit(solution)/shard_map/reduce_scatter | solution.py:646
  27.3 51.7 %copy-start.17 = (f32[768]{0:T(1024)}, f32[768]{0:T(1024)S(1)}, u32[]{:S(2)}) copy-start(f32[768]{0:T(1024)S(1)} %reshape.165) | copy-start | bytes 9220
  37.0 41.9 %copy-start.14 = (bf16[768,576]{1,0:T(8,128)(2,1)}, bf16[768,576]{1,0:T(8,128)(2,1)S(1)}, u32[]{:S(2)}) copy-start(bf16[768,576]{1,0:T(8,128)(2,1)S(1)} %all_gather.24) | copy-start | bytes 2654212
  72.0 2.8 copy-start.12
  74.9 4.1 %copy-start.20 = (f32[2048]{0:T(1024)}, f32[2048]{0:T(1024)S(1)}, u32[]{:S(2)}) copy-start(f32[2048]{0:T(1024)S(1)} %add_rsqrt_fusion) | copy-start | bytes 24580
  78.9 37.5 %copy-start.2 = (bf16[1,512,768]{2,1,0:T(8,128)(2,1)S(1)}, bf16[1,512,768]{2,1,0:T(8,128)(2,1)}, u32[]{:S(2)}) copy-start(bf16[1,512,768]{2,1,0:T(8,128)(2,1)} %param.10) | copy-start | bytes 2359300
  118.8 72.0 %copy-start.5 = (f32[512,768]{1,0:T(8,128)}, f32[512,768]{1,0:T(8,128)S(1)}, u32[]{:S(2)}) copy-start(f32[512,768]{1,0:T(8,128)S(1)} %get-tuple-element.63) | copy-start | bytes 4718596
  119.1 50.9 %copy-start.16 = (bf16[1,512,768]{2,1,0:T(8,128)(2,1)S(1)}, bf16[1,512,768]{2,1,0:T(8,128)(2,1)}, u32[]{:S(2)}) copy-start(bf16[1,512,768]{2,1,0:T(8,128)(2,1)} %param.19) | copy-start | bytes 2359300
  179.8 3.7 copy-start.4
  181.6 6.4 %slice-start.2 = ((s8[4718592]{0:T(1024)(128)(4,1)}), s8[4194304]{0:T(1024)(128)(4,1)S(1)}, s32[]{:S(2)}) async-start(s8[4718592]{0:T(1024)(128)(4,1)} %bitcast.123), calls=%async_computation.8 | async-start | bytes 8388608
  183.5 4.6 %slice-start.3 = ((s8[4718592]{0:T(1024)(128)(4,1)}), s8[524288]{0:T(1024)(128)(4,1)S(1)}, s32[]{:S(2)}) async-start(s8[4718592]{0:T(1024)(128)(4,1)} %bitcast.123), calls=%async_computation.9 | async-start | bytes 1048576
  192.0 1.8 copy-start
  192.0 2.1 copy-start.27
  307.2 1.9 copy-start.13
  307.2 1.9 copy-start.18
  307.2 1.9 copy-start.21
  375.7 5.5 %copy-start.10 = (bf16[192,2304]{1,0:T(8,128)(2,1)S(1)}, bf16[192,2304]{1,0:T(8,128)(2,1)}, u32[]{:S(2)}) copy-start(bf16[192,2304]{1,0:T(8,128)(2,1)} %param.12) | copy-start | bytes 2654212
  378.0 3.2 copy-start.11
  378.9 3.8 copy-start.7
  381.2 5.4 %slice-start = ((s8[6291456]{0:T(1024)(128)(4,1)}), s8[4194304]{0:T(1024)(128)(4,1)S(1)}, s32[]{:S(2)}) async-start(s8[6291456]{0:T(1024)(128)(4,1)} %bitcast.121), calls=%async_computation.6 | async-start | bytes 8388608
  382.7 4.0 slice-start.1
  384.4 2.2 copy-start.6
  386.6 6.0 %copy-start.3 = (bf16[1,512,768]{2,1,0:T(8,128)(2,1)S(1)}, bf16[1,512,768]{2,1,0:T(8,128)(2,1)}, u32[]{:S(2)}) copy-start(bf16[1,512,768]{2,1,0:T(8,128)(2,1)} %param.10) | copy-start | bytes 2359300
  (6 other events, 8.6 us)
Sparse Core Ops, SparseCore 0:
  9.6 62.4 all-gather.12
  73.6 18.2 all-gather.6
  93.4 37.4 all-gather.8
  132.4 37.5 all-gather.10
  307.3 70.4 reduce-scatter.1
